TPU v7x, 32 devices: a whole 2x2x4 slice. The times are simulated.
32 devices in a mesh: lines: 2 (over x), tile: 16 (over z, y, core).
Axes of the slice: x: 2, y: 2, z: 4, core: 2. Of those that a mesh axis runs over, the one named last changes fastest.
Arguments:
- traces: bfloat16 [1024, 512, 512], P(('lines', 'tile')), parts along dimension 0, may hold values from -6 to 6
Outputs:
- multiples: bfloat16 [1024, 512, 512], P(('lines', 'tile')), parts along dimension 0
There are 2 independent parts, one for each index of `lines`. A program takes and returns all parts, laid end to end along the dimension named above; each array names one. Nothing has to cross between parts.
All inputs are finite; a program needn't handle non-finite values.
Results may differ from a plain program's by a relative error of at most 0.011.
Values may be sent and summed in bfloat16 or wider, within the bound.
No kernel may reach another device: no remote copies, remote signals or barrier semaphores. Data moves between devices by JAX's collectives and lax.ppermute only.
A program may use at most 128 MiB of HBM per device.

v0:
```python
import math

import jax
import jax.numpy as jnp
import numpy as np
from jax import lax
from jax.experimental import pallas as pl
from jax.experimental.pallas import tpu as pltpu
from jax.sharding import Mesh
from jax.sharding import PartitionSpec as P

F = 128
VMEM = 60 << 20


def make_tables(nt):
    times = np.arange(nt, dtype=np.int64)
    freqs = np.arange(F, dtype=np.int64)
    angle = ((times[:, None] * freqs[None, :]) % nt).astype(np.float32) * np.float32(2.0 * math.pi / nt)
    norm = np.float32(1.0 / math.sqrt(nt))
    forward = np.stack([np.cos(angle), -np.sin(angle)], axis=-1) * norm
    weight = np.where(freqs == 0, 1.0, 2.0).astype(np.float32)
    inverse = np.stack([np.cos(angle).T * weight[:, None], -np.sin(angle).T * weight[:, None]], axis=1) * norm
    return forward.astype(jnp.bfloat16), inverse.astype(jnp.bfloat16)


def split(group):
    share = F // group
    chunks = math.gcd(4, share)
    return [share // chunks] * chunks


def grid_masks(size):
    row = lax.broadcasted_iota(jnp.int32, (size, size), 0)
    col = lax.broadcasted_iota(jnp.int32, (size, size), 1)
    return row, col


def forward_kernel(traces_ref, table_ref, *refs):
    outs, scratch = refs[:-1], refs[-1]
    rows = traces_ref.shape[0]
    count = table_ref.shape[0]
    for s in range(rows):
        value = lax.dot_general(
            table_ref[...], traces_ref[s], (((1,), (1,)), ((), ())), preferred_element_type=jnp.float32
        )
        for lane in range(scratch.shape[0]):
            scratch[lane, pl.ds(s, count, stride=rows), :] = value[:, lane * 128 : (lane + 1) * 128]
    at = 0
    for out in outs:
        n = out.shape[0]
        for lane in range(scratch.shape[0]):
            piece = scratch[lane, at * rows : (at + n) * rows, :].reshape(n, rows, 128)
            out[:, :, lane * 128 : (lane + 1) * 128] = piece.astype(jnp.bfloat16)
        at += n


def inverse_kernel(*refs):
    ins, table_ref, out_ref, scratch = refs[:-3], refs[-3], refs[-2], refs[-1]
    rows = out_ref.shape[0]
    count = table_ref.shape[0]
    at = 0
    for ref in ins:
        n = ref.shape[0]
        for lane in range(scratch.shape[0]):
            piece = ref[:, :, lane * 128 : (lane + 1) * 128].astype(jnp.float32)
            scratch[lane, at * rows : (at + n) * rows, :] = piece.reshape(n * rows, 128)
        at += n
    for s in range(rows):
        for lane in range(scratch.shape[0]):
            value = scratch[lane, pl.ds(s, count, stride=rows), :]
            value = lax.dot_general(
                value.T.astype(jnp.bfloat16), table_ref[...], (((1,), (0,)), ((), ())), preferred_element_type=jnp.float32
            )
            out_ref[s, lane * 128 : (lane + 1) * 128, :] = value.astype(jnp.bfloat16)


def transform(traces, table, counts):
    rows, size, nt = traces.shape
    total = table.shape[0]
    block = min(rows, 16)
    lanes = min(size, 256)
    return pl.pallas_call(
        forward_kernel,
        out_shape=tuple(jax.ShapeDtypeStruct((n, rows, size), jnp.bfloat16) for n in counts),
        grid=(rows // block, size // lanes),
        in_specs=[
            pl.BlockSpec((block, lanes, nt), lambda i, j: (i, j, 0)),
            pl.BlockSpec((total, nt), lambda i, j: (0, 0)),
        ],
        out_specs=tuple(pl.BlockSpec((n, block, lanes), lambda i, j: (0, i, j)) for n in counts),
        scratch_shapes=[pltpu.VMEM((lanes // 128, total * block, 128), jnp.float32)],
        compiler_params=pltpu.CompilerParams(vmem_limit_bytes=VMEM),
        cost_estimate=pl.CostEstimate(
            flops=2 * rows * size * nt * total, bytes_accessed=2 * rows * size * (nt + total), transcendentals=0
        ),
        name="transform",
    )(traces, table)


def restore(parts, table):
    rows, size = parts[0].shape[1:]
    total, nt = table.shape
    block = min(rows, 16)
    lanes = min(size, 256)
    return pl.pallas_call(
        inverse_kernel,
        out_shape=jax.ShapeDtypeStruct((rows, size, nt), jnp.bfloat16),
        grid=(rows // block, size // lanes),
        in_specs=[pl.BlockSpec((p.shape[0], block, lanes), lambda i, j: (0, i, j)) for p in parts]
        + [pl.BlockSpec((total, nt), lambda i, j: (0, 0))],
        out_specs=pl.BlockSpec((block, lanes, nt), lambda i, j: (i, j, 0)),
        scratch_shapes=[pltpu.VMEM((lanes // 128, total * block, 128), jnp.float32)],
        compiler_params=pltpu.CompilerParams(vmem_limit_bytes=VMEM),
        cost_estimate=pl.CostEstimate(
            flops=2 * rows * size * nt * total, bytes_accessed=2 * rows * size * (nt + total), transcendentals=0
        ),
        name="restore",
    )(*parts, table)


def pack_kernel(half_ref, mine_ref, own_ref, sent_ref):
    size = own_ref.shape[2]
    half = half_ref[0]
    near = pl.multiple_of(half * size, size)
    far = pl.multiple_of((1 - half) * size, size)
    own = []
    for c in range(2):
        block = mine_ref[:, 0, c, :, pl.ds(near, size)].reshape(size, size).astype(jnp.float32)
        own.append(((block + block.T) * 0.5).astype(jnp.bfloat16))
        own_ref[0, c] = own[c]
        sent_ref[0, c * size : (c + 1) * size] = mine_ref[:, 0, c, :, pl.ds(far, size)].reshape(size, size)
    row, col = grid_masks(size)
    real, imag = own[0].astype(jnp.float32), own[1].astype(jnp.float32)
    sent_ref[0, 2 * size : 3 * size] = jnp.where(row <= col, real, imag).astype(jnp.bfloat16)
    diagonal = jnp.sum(jnp.where(row == col, imag, 0.0), axis=0, keepdims=True)
    tail = sent_ref.shape[1] - 3 * size
    sent_ref[0, 3 * size :] = jnp.broadcast_to(diagonal, (tail, size)).astype(jnp.bfloat16)


def product_kernel(half_ref, own_ref, sent_ref, got_ref, out_ref, lhs_ref, rhs_ref, sum_ref):
    group, rows, full = out_ref.shape[0], out_ref.shape[3], out_ref.shape[4]
    size = full // 2
    eta = 1.0 / math.sqrt(full)
    half = half_ref[0]
    near = pl.multiple_of(half * size, size)
    far = pl.multiple_of((1 - half) * size, size)
    row, col = grid_masks(size)
    packed = got_ref[0, 2 * size : 3 * size].astype(jnp.float32)
    turned = packed.T
    diagonal = got_ref[0, 3 * size :].astype(jnp.float32)[0:1]
    there = (
        jnp.where(row <= col, packed, turned),
        jnp.where(row > col, packed, jnp.where(row < col, turned, diagonal)),
    )
    for c in range(2):
        at = slice(c * size, (c + 1) * size)
        mixed = (sent_ref[0, at].astype(jnp.float32) + got_ref[0, at].astype(jnp.float32).T) * 0.5
        mixed = mixed.astype(jnp.bfloat16)
        turned = mixed.astype(jnp.float32).T.astype(jnp.bfloat16)
        base = c * full
        rhs_ref[base : base + size, 0:size] = own_ref[0, c]
        rhs_ref[base : base + size, size:full] = mixed
        rhs_ref[base + size : base + full, 0:size] = turned
        rhs_ref[base + size : base + full, size:full] = there[c].astype(jnp.bfloat16)
    lhs_ref[0:full, 0:full] = rhs_ref[0:full]
    lhs_ref[full:, full:] = rhs_ref[0:full]
    lhs_ref[full:, 0:full] = rhs_ref[full:]
    lhs_ref[0:full, full:] = -rhs_ref[full:]

    @pl.loop(0, 4)
    def _(step):
        at = pl.ds(pl.multiple_of(step * size, size), size)
        square = jnp.dot(lhs_ref[at, :], rhs_ref[...], preferred_element_type=jnp.float32)
        sum_ref[at, :] = (rhs_ref[at, :].astype(jnp.float32) + eta * square).astype(jnp.bfloat16)

    for c in range(2):
        value = jnp.dot(lhs_ref[c * full : c * full + size], sum_ref[...], preferred_element_type=jnp.float32)
        value = (eta * value).astype(jnp.bfloat16).reshape(group, rows, full)
        out_ref[:, 0, c, :, pl.ds(near, size)] = value[:, :, 0:size]
        out_ref[:, 0, c, :, pl.ds(far, size)] = value[:, :, size:full]


def pack(half, mine):
    group, count, _, rows, full = mine.shape
    size = full // 2
    sent = 3 * size + 16
    return pl.pallas_call(
        pack_kernel,
        out_shape=(
            jax.ShapeDtypeStruct((count, 2, size, size), jnp.bfloat16),
            jax.ShapeDtypeStruct((count, sent, size), jnp.bfloat16),
        ),
        grid_spec=pltpu.PrefetchScalarGridSpec(
            num_scalar_prefetch=1,
            grid=(count,),
            in_specs=[pl.BlockSpec((group, 1, 2, rows, full), lambda k, h: (0, k, 0, 0, 0))],
            out_specs=[
                pl.BlockSpec((1, 2, size, size), lambda k, h: (k, 0, 0, 0)),
                pl.BlockSpec((1, sent, size), lambda k, h: (k, 0, 0)),
            ],
        ),
        compiler_params=pltpu.CompilerParams(vmem_limit_bytes=VMEM),
        cost_estimate=pl.CostEstimate(flops=count * size * size * 8, bytes_accessed=count * full * full * 5, transcendentals=0),
        name="pack",
    )(half, mine)


def products(half, own, sent, got, group):
    count, size = own.shape[0], own.shape[2]
    full = 2 * size
    rows = size // group
    shape = jax.ShapeDtypeStruct((group, count, 2, rows, full), jnp.bfloat16)
    passed = pl.BlockSpec((1,) + got.shape[1:], lambda k, h: (k, 0, 0))
    return pl.pallas_call(
        product_kernel,
        out_shape=shape,
        grid_spec=pltpu.PrefetchScalarGridSpec(
            num_scalar_prefetch=1,
            grid=(count,),
            in_specs=[pl.BlockSpec((1, 2, size, size), lambda k, h: (k, 0, 0, 0)), passed, passed],
            out_specs=pl.BlockSpec((group, 1, 2, rows, full), lambda k, h: (0, k, 0, 0, 0)),
            scratch_shapes=[
                pltpu.VMEM((2 * full, 2 * full), jnp.bfloat16),
                pltpu.VMEM((2 * full, full), jnp.bfloat16),
                pltpu.VMEM((2 * full, full), jnp.bfloat16),
            ],
        ),
        compiler_params=pltpu.CompilerParams(vmem_limit_bytes=VMEM),
        cost_estimate=pl.CostEstimate(flops=count * full**3 * 12, bytes_accessed=count * full * full * 5, transcendentals=0),
        name="products",
    )(half, own, sent, got)


def local(group, traces):
    rows, size, nt = traces.shape
    flag = lax.axis_index("half").astype(jnp.int32).reshape(1)
    chunks = split(group)
    forward, inverse = make_tables(nt)
    table = forward.reshape(nt, 2 * F).T
    spectra = transform(traces, jnp.asarray(table), [2 * group * n for n in chunks])
    parts = []
    for n, spectrum in zip(chunks, spectra):
        spectrum = spectrum.reshape(group, n, 2, rows, size)
        mine = lax.all_to_all(spectrum, "member", split_axis=0, concat_axis=0, tiled=True)
        own, sent = pack(flag, mine)
        got = lax.ppermute(sent, "half", [(0, 1), (1, 0)])
        predicted = products(flag, own, sent, got, group)
        returned = lax.all_to_all(predicted, "member", split_axis=0, concat_axis=0, tiled=True)
        parts.append(returned.reshape(group * n * 2, rows, size))
    return restore(parts, jnp.asarray(inverse.reshape(2 * F, nt)))


def solution(mesh):
    lines, count = mesh.shape["lines"], mesh.shape["tile"]
    group = count // 2
    inside = Mesh(mesh.devices.reshape(lines, 2, group), ("lines", "half", "member"))
    spec = P(inside.axis_names, None, None)

    def body(traces):
        return local(group, traces)

    return jax.shard_map(body, mesh=inside, in_specs=(spec,), out_specs=spec, check_vma=False)
```

profile of v0, /device:TPU:15, one launch (start us, length us, event | category | flops | bytes accessed | tf_op | source)
XLA Modules:
  0.0 531.4 jit_solution(8114653011294134643)
XLA Ops:
  0.0 13.4 %transform.1 = (bf16[64,32,512]{2,1,0:T(8,128)(2,1)}, bf16[64,32,512]{2,1,0:T(8,128)(2,1)}, bf16[64,32,512]{2,1,0:T(8,128)(2,1)}, bf16[64,32,512]{2,1,0:T(8,128)(2,1)}) custom-call(bf16[32,512,512]{2,1,0:T(8,128)(2,1)} %traces_ref.1, bf16[256,512]{1,0:T(8,128)(2,1)} %constant.10.clone.table_ref), custom_call_target="tpu_custom_call" | custom-call | flops 4294967296 | bytes 25165824 | tf_op jit(solution)/shard_map/transform/pallas_call | solution.py:83
  13.4 29.3 %all_to_all.40.mine_ref = bf16[8,4,2,32,512]{4,3,2,1,0:T(8,128)(2,1)} all-to-all(bf16[8,4,2,32,512]{4,3,2,1,0:T(8,128)(2,1)} %bitcast.15), channel_id=1, replica_groups=mesh['lines'=2,'half'=2,'member'=8] {'member'}, dimensions={0} | all-to-all | bytes 4194304 | tf_op jit(solution)/shard_map/all_to_all | solution.py:245
  42.7 29.3 %all_to_all.41.mine_ref = bf16[8,4,2,32,512]{4,3,2,1,0:T(8,128)(2,1)} all-to-all(bf16[8,4,2,32,512]{4,3,2,1,0:T(8,128)(2,1)S(1)} %bitcast.14), channel_id=1, replica_groups=mesh['lines'=2,'half'=2,'member'=8] {'member'}, dimensions={0} | all-to-all | bytes 4194304 | tf_op jit(solution)/shard_map/all_to_all | solution.py:245
  72.0 29.2 %all_to_all.42.mine_ref = bf16[8,4,2,32,512]{4,3,2,1,0:T(8,128)(2,1)} all-to-all(bf16[8,4,2,32,512]{4,3,2,1,0:T(8,128)(2,1)S(1)} %bitcast.13), channel_id=1, replica_groups=mesh['lines'=2,'half'=2,'member'=8] {'member'}, dimensions={0} | all-to-all | bytes 4194304 | tf_op jit(solution)/shard_map/all_to_all | solution.py:245
  101.2 5.4 %all-to-all-start.6 = ((bf16[8,4,2,32,512]{4,3,2,1,0:T(8,128)(2,1)}), bf16[8,4,2,32,512]{4,3,2,1,0:T(8,128)(2,1)S(1)}, u32[]{:S(2)}, u32[]{:S(2)}) async-start(bf16[8,4,2,32,512]{4,3,2,1,0:T(8,128)(2,1)} %bitcast.12), calls=%async_computation.6 | async-start | bytes 4194304 | tf_op jit(solution)/shard_map/all_to_all | solution.py:245
  106.6 4.2 pack.5
  110.7 2.3 collective-permute-start.1
  113.0 68.8 %collective-permute-done.1.got_ref = bf16[4,784,256]{2,1,0:T(8,128)(2,1)} collective-permute-done((bf16[4,784,256]{2,1,0:T(8,128)(2,1)}, bf16[4,784,256]{2,1,0:T(8,128)(2,1)}, u32[]{:S(2)}, u32[]{:S(2)}) %collective-permute-start.1) | collective-permute-done | bytes 1605664 | tf_op jit(solution)/shard_map/ppermute | solution.py:247
  181.9 13.7 %products.5 = bf16[8,4,2,32,512]{4,3,2,1,0:T(8,128)(2,1)} custom-call(s32[1]{0:T(128)} %bitcast.half_ref, bf16[4,2,256,256]{3,2,1,0:T(8,128)(2,1)} %get-tuple-element.21.own_ref, bf16[4,784,256]{2,1,0:T(8,128)(2,1)} %get-tuple-element.22.sent_ref, bf16[4,784,256]{2,1,0:T(8,128)(2,1)} %collective-permute-done.1.got_ref), custom_call_target="tpu_custom_call" | custom-call | flops 6442450944 | bytes 5242880 | tf_op jit(solution)/shard_map/products/pallas_call | solution.py:215
  197.0 5.5 %all-to-all-start.3 = ((bf16[8,4,2,32,512]{4,3,2,1,0:T(8,128)(2,1)}), bf16[8,4,2,32,512]{4,3,2,1,0:T(8,128)(2,1)S(1)}, u32[]{:S(2)}, u32[]{:S(2)}) async-start(bf16[8,4,2,32,512]{4,3,2,1,0:T(8,128)(2,1)} %products.5), calls=%async_computation.3 | async-start | bytes 4194304 | tf_op jit(solution)/shard_map/all_to_all | solution.py:249
  202.5 4.2 pack.4
  206.7 2.6 collective-permute-start
  209.3 68.8 %collective-permute-done.got_ref = bf16[4,784,256]{2,1,0:T(8,128)(2,1)} collective-permute-done((bf16[4,784,256]{2,1,0:T(8,128)(2,1)}, bf16[4,784,256]{2,1,0:T(8,128)(2,1)}, u32[]{:S(2)}, u32[]{:S(2)}) %collective-permute-start) | collective-permute-done | bytes 1605664 | tf_op jit(solution)/shard_map/ppermute | solution.py:247
  278.1 13.7 %products.4 = bf16[8,4,2,32,512]{4,3,2,1,0:T(8,128)(2,1)} custom-call(s32[1]{0:T(128)} %bitcast.half_ref, bf16[4,2,256,256]{3,2,1,0:T(8,128)(2,1)} %get-tuple-element.18.own_ref, bf16[4,784,256]{2,1,0:T(8,128)(2,1)} %get-tuple-element.19.sent_ref, bf16[4,784,256]{2,1,0:T(8,128)(2,1)} %collective-permute-done.got_ref), custom_call_target="tpu_custom_call" | custom-call | flops 6442450944 | bytes 5242880 | tf_op jit(solution)/shard_map/products/pallas_call | solution.py:215
  293.2 6.3 %all-to-all-start.1 = ((bf16[8,4,2,32,512]{4,3,2,1,0:T(8,128)(2,1)}), bf16[8,4,2,32,512]{4,3,2,1,0:T(8,128)(2,1)}, u32[]{:S(2)}, u32[]{:S(2)}) async-start(bf16[8,4,2,32,512]{4,3,2,1,0:T(8,128)(2,1)} %products.4), calls=%async_computation.1 | async-start | bytes 4194304 | tf_op jit(solution)/shard_map/all_to_all | solution.py:249
  299.4 4.2 pack.6
  305.6 68.7 %collective-permute-done.2.got_ref = bf16[4,784,256]{2,1,0:T(8,128)(2,1)S(1)} collective-permute-done((bf16[4,784,256]{2,1,0:T(8,128)(2,1)}, bf16[4,784,256]{2,1,0:T(8,128)(2,1)S(1)}, u32[]{:S(2)}, u32[]{:S(2)}) %collective-permute-start.2) | collective-permute-done | bytes 1605664 | tf_op jit(solution)/shard_map/ppermute | solution.py:247
  375.4 13.7 %products.6 = bf16[8,4,2,32,512]{4,3,2,1,0:T(8,128)(2,1)} custom-call(s32[1]{0:T(128)} %bitcast.half_ref, bf16[4,2,256,256]{3,2,1,0:T(8,128)(2,1)} %get-tuple-element.24.own_ref, bf16[4,784,256]{2,1,0:T(8,128)(2,1)} %get-tuple-element.25.sent_ref, bf16[4,784,256]{2,1,0:T(8,128)(2,1)} %copy-done.5), custom_call_target="tpu_custom_call" | custom-call | flops 6442450944 | bytes 5242880 | tf_op jit(solution)/shard_map/products/pallas_call | solution.py:215
  389.2 6.0 %all-to-all-start.5 = ((bf16[8,4,2,32,512]{4,3,2,1,0:T(8,128)(2,1)}), bf16[8,4,2,32,512]{4,3,2,1,0:T(8,128)(2,1)S(1)}, u32[]{:S(2)}, u32[]{:S(2)}) async-start(bf16[8,4,2,32,512]{4,3,2,1,0:T(8,128)(2,1)} %products.6), calls=%async_computation.5 | async-start | bytes 4194304 | tf_op jit(solution)/shard_map/all_to_all | solution.py:249
  395.1 4.2 pack.7
  401.6 68.8 %collective-permute-done.3.got_ref = bf16[4,784,256]{2,1,0:T(8,128)(2,1)} collective-permute-done((bf16[4,784,256]{2,1,0:T(8,128)(2,1)}, bf16[4,784,256]{2,1,0:T(8,128)(2,1)}, u32[]{:S(2)}, u32[]{:S(2)}) %collective-permute-start.3) | collective-permute-done | bytes 1605664 | tf_op jit(solution)/shard_map/ppermute | solution.py:247
  470.4 13.7 %products.7 = bf16[8,4,2,32,512]{4,3,2,1,0:T(8,128)(2,1)} custom-call(s32[1]{0:T(128)} %bitcast.half_ref, bf16[4,2,256,256]{3,2,1,0:T(8,128)(2,1)} %get-tuple-element.27.own_ref, bf16[4,784,256]{2,1,0:T(8,128)(2,1)} %get-tuple-element.28.sent_ref, bf16[4,784,256]{2,1,0:T(8,128)(2,1)} %collective-permute-done.3.got_ref), custom_call_target="tpu_custom_call" | custom-call | flops 6442450944 | bytes 5242880 | tf_op jit(solution)/shard_map/products/pallas_call | solution.py:215
  484.1 30.6 %all_to_all.43 = bf16[8,4,2,32,512]{4,3,2,1,0:T(8,128)(2,1)} all-to-all(bf16[8,4,2,32,512]{4,3,2,1,0:T(8,128)(2,1)} %products.7), channel_id=1, replica_groups=mesh['lines'=2,'half'=2,'member'=8] {'member'}, dimensions={0} | all-to-all | bytes 4194304 | tf_op jit(solution)/shard_map/all_to_all | solution.py:249
  514.7 16.7 %restore.1 = bf16[32,512,512]{2,1,0:T(8,128)(2,1)} custom-call(bf16[64,32,512]{2,1,0:T(8,128)(2,1)} %bitcast.2.refs_0_, bf16[64,32,512]{2,1,0:T(8,128)(2,1)} %bitcast.9, bf16[64,32,512]{2,1,0:T(8,128)(2,1)} %bitcast.10, bf16[64,32,512]{2,1,0:T(8,128)(2,1)} %bitcast.11, bf16[256,512]{1,0:T(8,128)(2,1)} %constant.11.clone.refs_4_), custom_call_target="tpu_custom_call" | custom-call | flops 4294967296 | bytes 25165824 | tf_op jit(solution)/shard_map/restore/pallas_call | solution.py:106
  (18 shorter events, 8.0 us)
Async XLA Ops:
  13.4 29.3 %copy-start.4 = (bf16[64,32,512]{2,1,0:T(8,128)(2,1)S(1)}, bf16[64,32,512]{2,1,0:T(8,128)(2,1)}, u32[]{:S(2)}) copy-start(bf16[64,32,512]{2,1,0:T(8,128)(2,1)} %get-tuple-element.17) | copy-start | bytes 6291460
  42.7 29.3 %copy-start.3 = (bf16[64,32,512]{2,1,0:T(8,128)(2,1)S(1)}, bf16[64,32,512]{2,1,0:T(8,128)(2,1)}, u32[]{:S(2)}) copy-start(bf16[64,32,512]{2,1,0:T(8,128)(2,1)} %get-tuple-element.23) | copy-start | bytes 6291460
  101.2 94.4 %all-to-all-start.6 = ((bf16[8,4,2,32,512]{4,3,2,1,0:T(8,128)(2,1)}), bf16[8,4,2,32,512]{4,3,2,1,0:T(8,128)(2,1)S(1)}, u32[]{:S(2)}, u32[]{:S(2)}) async-start(bf16[8,4,2,32,512]{4,3,2,1,0:T(8,128)(2,1)} %bitcast.12), calls=%async_computation.6 | async-start | bytes 4194304 | tf_op jit(solution)/shard_map/all_to_all | solution.py:245
  110.7 71.1 %collective-permute-start.1 = (bf16[4,784,256]{2,1,0:T(8,128)(2,1)}, bf16[4,784,256]{2,1,0:T(8,128)(2,1)}, u32[]{:S(2)}, u32[]{:S(2)}) collective-permute-start(bf16[4,784,256]{2,1,0:T(8,128)(2,1)} %get-tuple-element.22.sent_ref), channel_id=1, source_target_pairs={{0,8},{8,0},{1,9},{9,1},{2,10},{10,2},{3,11},{11,3},{4,12},{12,4},... | collective-permute-start | bytes 4816904 | tf_op jit(solution)/shard_map/ppermute | solution.py:247
  195.6 1.4 copy-start.2
  197.0 94.9 %all-to-all-start.3 = ((bf16[8,4,2,32,512]{4,3,2,1,0:T(8,128)(2,1)}), bf16[8,4,2,32,512]{4,3,2,1,0:T(8,128)(2,1)S(1)}, u32[]{:S(2)}, u32[]{:S(2)}) async-start(bf16[8,4,2,32,512]{4,3,2,1,0:T(8,128)(2,1)} %products.5), calls=%async_computation.3 | async-start | bytes 4194304 | tf_op jit(solution)/shard_map/all_to_all | solution.py:249
  206.7 71.4 %collective-permute-start = (bf16[4,784,256]{2,1,0:T(8,128)(2,1)}, bf16[4,784,256]{2,1,0:T(8,128)(2,1)}, u32[]{:S(2)}, u32[]{:S(2)}) collective-permute-start(bf16[4,784,256]{2,1,0:T(8,128)(2,1)} %get-tuple-element.19.sent_ref), channel_id=1, source_target_pairs={{0,8},{8,0},{1,9},{9,1},{2,10},{10,2},{3,11},{11,3},{4,12},{12,4},... | collective-permute-start | bytes 4816904 | tf_op jit(solution)/shard_map/ppermute | solution.py:247
  291.8 1.3 copy-start
  293.2 96.0 %all-to-all-start.1 = ((bf16[8,4,2,32,512]{4,3,2,1,0:T(8,128)(2,1)}), bf16[8,4,2,32,512]{4,3,2,1,0:T(8,128)(2,1)}, u32[]{:S(2)}, u32[]{:S(2)}) async-start(bf16[8,4,2,32,512]{4,3,2,1,0:T(8,128)(2,1)} %products.4), calls=%async_computation.1 | async-start | bytes 4194304 | tf_op jit(solution)/shard_map/all_to_all | solution.py:249
  303.7 70.6 %collective-permute-start.2 = (bf16[4,784,256]{2,1,0:T(8,128)(2,1)}, bf16[4,784,256]{2,1,0:T(8,128)(2,1)S(1)}, u32[]{:S(2)}, u32[]{:S(2)}) collective-permute-start(bf16[4,784,256]{2,1,0:T(8,128)(2,1)} %get-tuple-element.25.sent_ref), channel_id=1, source_target_pairs={{0,8},{8,0},{1,9},{9,1},{2,10},{10,2},{3,11},{11,3},{4,12},{12,4},... | collective-permute-start | bytes 4816904 | tf_op jit(solution)/shard_map/ppermute | solution.py:247
  374.3 1.2 copy-start.5
  389.2 94.9 %all-to-all-start.5 = ((bf16[8,4,2,32,512]{4,3,2,1,0:T(8,128)(2,1)}), bf16[8,4,2,32,512]{4,3,2,1,0:T(8,128)(2,1)S(1)}, u32[]{:S(2)}, u32[]{:S(2)}) async-start(bf16[8,4,2,32,512]{4,3,2,1,0:T(8,128)(2,1)} %products.6), calls=%async_computation.5 | async-start | bytes 4194304 | tf_op jit(solution)/shard_map/all_to_all | solution.py:249
  399.4 71.0 %collective-permute-start.3 = (bf16[4,784,256]{2,1,0:T(8,128)(2,1)}, bf16[4,784,256]{2,1,0:T(8,128)(2,1)}, u32[]{:S(2)}, u32[]{:S(2)}) collective-permute-start(bf16[4,784,256]{2,1,0:T(8,128)(2,1)} %get-tuple-element.28.sent_ref), channel_id=1, source_target_pairs={{0,8},{8,0},{1,9},{9,1},{2,10},{10,2},{3,11},{11,3},{4,12},{12,4},... | collective-permute-start | bytes 4816904 | tf_op jit(solution)/shard_map/ppermute | solution.py:247
  484.1 30.6 %copy-start.1 = (bf16[8,4,2,32,512]{4,3,2,1,0:T(8,128)(2,1)}, bf16[8,4,2,32,512]{4,3,2,1,0:T(8,128)(2,1)S(1)}, u32[]{:S(2)}) copy-start(bf16[8,4,2,32,512]{4,3,2,1,0:T(8,128)(2,1)S(1)} %all-to-all-done.5) | copy-start | bytes 6291460
where the time goes:
time: 535 us; the launch traced here: 531 us
  waiting for transfers between devices  275 us (51%)
  blocking collectives  118 us (22%)
  Pallas kernels  102 us (19%)
  starting transfers between devices  32.2 us (6%)
    ppermute x4, waiting for transfers between devices, local(): got = lax.ppermute(sent, 'half', [(0, 1), (1, 0)])  275 us
    all_to_all x3, blocking collectives, local(): lax.all_to_all(spectrum, 'member', split_axis=0, concat_axis=0, tiled=True)  87.8 us
    pallas_call x4, Pallas kernels, products(): pl.pallas_call(product_kernel, out_shape=shape, grid_spec=pltpu.PrefetchS...  54.9 us
    all_to_all x1, blocking collectives, local(): lax.all_to_all(predicted, 'member', split_axis=0, concat_axis=0, tiled=True)  30.6 us
    all_to_all x3, starting transfers between devices, local(): lax.all_to_all(predicted, 'member', split_axis=0, concat_axis=0, tiled=True)  17.8 us
    pallas_call x4, Pallas kernels, pack(): pl.pallas_call(pack_kernel, out_shape=(jax.ShapeDtypeStruct((count, 2, si...  16.8 us
    pallas_call x1, Pallas kernels, restore(): pl.pallas_call(inverse_kernel, out_shape=jax.ShapeDtypeStruct((rows, size...  16.7 us
    pallas_call x1, Pallas kernels, transform(): pl.pallas_call(forward_kernel, out_shape=tuple((jax.ShapeDtypeStruct((n,...  13.4 us
  transfers between devices with their start and end apart: 8, of which 4 were waited for; matrix products, arithmetic and copies ran while one was open for 0% of the time, Pallas kernels for 13%

commit v1 on v0

--- a/solution.py
+++ b/solution.py
@@ -11,6 +11,8 @@
 
 F = 128
 VMEM = 60 << 20
+TAIL = 16
+SIZES = (3, 4, 5, 4, 16)
 
 
 def make_tables(nt):
@@ -26,8 +28,8 @@
 
 def split(group):
     share = F // group
-    chunks = math.gcd(4, share)
-    return [share // chunks] * chunks
+    marks = [round(share * mark / SIZES[-1]) for mark in np.cumsum((0,) + SIZES[:-1])]
+    return [b - a for a, b in zip(marks, marks[1:]) if b > a]
 
 
 def grid_masks(size):
@@ -67,12 +69,9 @@
             scratch[lane, at * rows : (at + n) * rows, :] = piece.reshape(n * rows, 128)
         at += n
     for s in range(rows):
-        for lane in range(scratch.shape[0]):
-            value = scratch[lane, pl.ds(s, count, stride=rows), :]
-            value = lax.dot_general(
-                value.T.astype(jnp.bfloat16), table_ref[...], (((1,), (0,)), ((), ())), preferred_element_type=jnp.float32
-            )
-            out_ref[s, lane * 128 : (lane + 1) * 128, :] = value.astype(jnp.bfloat16)
+        lanes = [scratch[lane, pl.ds(s, count, stride=rows), :] for lane in range(scratch.shape[0])]
+        value = jnp.concatenate(lanes, axis=1).T.astype(jnp.bfloat16)
+        out_ref[s] = jnp.dot(value, table_ref[...], preferred_element_type=jnp.float32).astype(jnp.bfloat16)
 
 
 def transform(traces, table, counts):
@@ -124,18 +123,24 @@
     half = half_ref[0]
     near = pl.multiple_of(half * size, size)
     far = pl.multiple_of((1 - half) * size, size)
+    step = pl.program_id(0)
+    base = step * (3 * size)
     own = []
     for c in range(2):
         block = mine_ref[:, 0, c, :, pl.ds(near, size)].reshape(size, size).astype(jnp.float32)
         own.append(((block + block.T) * 0.5).astype(jnp.bfloat16))
         own_ref[0, c] = own[c]
-        sent_ref[0, c * size : (c + 1) * size] = mine_ref[:, 0, c, :, pl.ds(far, size)].reshape(size, size)
+        at = pl.ds(pl.multiple_of(base + c * size, size), size)
+        sent_ref[at] = mine_ref[:, 0, c, :, pl.ds(far, size)].reshape(size, size)
     row, col = grid_masks(size)
     real, imag = own[0].astype(jnp.float32), own[1].astype(jnp.float32)
-    sent_ref[0, 2 * size : 3 * size] = jnp.where(row <= col, real, imag).astype(jnp.bfloat16)
+    at = pl.ds(pl.multiple_of(base + 2 * size, size), size)
+    sent_ref[at] = jnp.where(row <= col, real, imag).astype(jnp.bfloat16)
     diagonal = jnp.sum(jnp.where(row == col, imag, 0.0), axis=0, keepdims=True)
-    tail = sent_ref.shape[1] - 3 * size
-    sent_ref[0, 3 * size :] = jnp.broadcast_to(diagonal, (tail, size)).astype(jnp.bfloat16)
+    tail = sent_ref.shape[0] - TAIL
+    line = lax.broadcasted_iota(jnp.int32, (TAIL, size), 0)
+    before = jnp.where(step == 0, 0.0, sent_ref[tail:].astype(jnp.float32))
+    sent_ref[tail:] = jnp.where(line == step, diagonal, before).astype(jnp.bfloat16)
 
 
 def product_kernel(half_ref, own_ref, sent_ref, got_ref, out_ref, lhs_ref, rhs_ref, sum_ref):
@@ -146,16 +151,20 @@
     near = pl.multiple_of(half * size, size)
     far = pl.multiple_of((1 - half) * size, size)
     row, col = grid_masks(size)
-    packed = got_ref[0, 2 * size : 3 * size].astype(jnp.float32)
+    step = pl.program_id(0)
+    start = step * (3 * size)
+    packed = got_ref[pl.ds(pl.multiple_of(start + 2 * size, size), size)].astype(jnp.float32)
     turned = packed.T
-    diagonal = got_ref[0, 3 * size :].astype(jnp.float32)[0:1]
+    tail = got_ref[got_ref.shape[0] - TAIL :].astype(jnp.float32)
+    line = lax.broadcasted_iota(jnp.int32, (TAIL, size), 0)
+    diagonal = jnp.sum(jnp.where(line == step, tail, 0.0), axis=0, keepdims=True)
     there = (
         jnp.where(row <= col, packed, turned),
         jnp.where(row > col, packed, jnp.where(row < col, turned, diagonal)),
     )
     for c in range(2):
-        at = slice(c * size, (c + 1) * size)
-        mixed = (sent_ref[0, at].astype(jnp.float32) + got_ref[0, at].astype(jnp.float32).T) * 0.5
+        at = pl.ds(pl.multiple_of(start + c * size, size), size)
+        mixed = (sent_ref[at].astype(jnp.float32) + got_ref[at].astype(jnp.float32).T) * 0.5
         mixed = mixed.astype(jnp.bfloat16)
         turned = mixed.astype(jnp.float32).T.astype(jnp.bfloat16)
         base = c * full
@@ -169,8 +178,8 @@
     lhs_ref[0:full, full:] = -rhs_ref[full:]
 
     @pl.loop(0, 4)
-    def _(step):
-        at = pl.ds(pl.multiple_of(step * size, size), size)
+    def _(part):
+        at = pl.ds(pl.multiple_of(part * size, size), size)
         square = jnp.dot(lhs_ref[at, :], rhs_ref[...], preferred_element_type=jnp.float32)
         sum_ref[at, :] = (rhs_ref[at, :].astype(jnp.float32) + eta * square).astype(jnp.bfloat16)
 
@@ -184,12 +193,12 @@
 def pack(half, mine):
     group, count, _, rows, full = mine.shape
     size = full // 2
-    sent = 3 * size + 16
+    sent = count * 3 * size + TAIL
     return pl.pallas_call(
         pack_kernel,
         out_shape=(
             jax.ShapeDtypeStruct((count, 2, size, size), jnp.bfloat16),
-            jax.ShapeDtypeStruct((count, sent, size), jnp.bfloat16),
+            jax.ShapeDtypeStruct((sent, size), jnp.bfloat16),
         ),
         grid_spec=pltpu.PrefetchScalarGridSpec(
             num_scalar_prefetch=1,
@@ -197,7 +206,7 @@
             in_specs=[pl.BlockSpec((group, 1, 2, rows, full), lambda k, h: (0, k, 0, 0, 0))],
             out_specs=[
                 pl.BlockSpec((1, 2, size, size), lambda k, h: (k, 0, 0, 0)),
-                pl.BlockSpec((1, sent, size), lambda k, h: (k, 0, 0)),
+                pl.BlockSpec((sent, size), lambda k, h: (0, 0)),
             ],
         ),
         compiler_params=pltpu.CompilerParams(vmem_limit_bytes=VMEM),
@@ -211,7 +220,7 @@
     full = 2 * size
     rows = size // group
     shape = jax.ShapeDtypeStruct((group, count, 2, rows, full), jnp.bfloat16)
-    passed = pl.BlockSpec((1,) + got.shape[1:], lambda k, h: (k, 0, 0))
+    passed = pl.BlockSpec(got.shape, lambda k, h: (0, 0))
     return pl.pallas_call(
         product_kernel,
         out_shape=shape,
@@ -238,7 +247,9 @@
     chunks = split(group)
     forward, inverse = make_tables(nt)
     table = forward.reshape(nt, 2 * F).T
-    spectra = transform(traces, jnp.asarray(table), [2 * group * n for n in chunks])
+    counts = [2 * group * n for n in chunks]
+    spectra = transform(traces, jnp.asarray(table[: counts[0]]), counts[:1])
+    spectra += transform(traces, jnp.asarray(table[counts[0] :]), counts[1:])
     parts = []
     for n, spectrum in zip(chunks, spectra):
         spectrum = spectrum.reshape(group, n, 2, rows, size)

time: 535 us -> 531 us (level)
  blocking collectives: 118 us -> 96.7 us
  Pallas kernels: 102 us -> 114 us
    all_to_all x3 -> x2, blocking collectives: 87.8 us -> 59.9 us  [local(): lax.all_to_all(spectrum, 'member', split_axis=0, concat_axis=0, tiled=True)]
    pallas_call x1 -> x2, Pallas kernels: 13.4 us -> 22.8 us  [transform(): pl.pallas_call(forward_kernel, out_shape=tuple((jax.ShapeDtypeStruct((n,...]
    all_to_all x1, blocking collectives: 30.6 us -> 36.7 us  [local(): lax.all_to_all(predicted, 'member', split_axis=0, concat_axis=0, tiled=True)]
  transfers between devices with their start and end apart: 8 -> 9, of which waited for: 4 -> 5; matrix products, arithmetic and copies ran while one was open for 0% -> 0% of each run, Pallas kernels for 13% -> 17%
where the time goes in v1:
time: 531 us; the launch traced here: 527 us
  waiting for transfers between devices  276 us (52%)
  Pallas kernels  114 us (21%)
  blocking collectives  96.7 us (18%)
  starting transfers between devices  36.7 us (7%)
    ppermute x4, waiting for transfers between devices, local(): got = lax.ppermute(sent, 'half', [(0, 1), (1, 0)])  271 us
    all_to_all x2, blocking collectives, local(): lax.all_to_all(spectrum, 'member', split_axis=0, concat_axis=0, tiled=True)  59.9 us
    pallas_call x4, Pallas kernels, products(): pl.pallas_call(product_kernel, out_shape=shape, grid_spec=pltpu.PrefetchS...  57.9 us
    all_to_all x1, blocking collectives, local(): lax.all_to_all(predicted, 'member', split_axis=0, concat_axis=0, tiled=True)  36.7 us
    pallas_call x2, Pallas kernels, transform(): pl.pallas_call(forward_kernel, out_shape=tuple((jax.ShapeDtypeStruct((n,...  22.8 us
    all_to_all x3, starting transfers between devices, local(): lax.all_to_all(predicted, 'member', split_axis=0, concat_axis=0, tiled=True)  18.4 us
    pallas_call x4, Pallas kernels, pack(): pl.pallas_call(pack_kernel, out_shape=(jax.ShapeDtypeStruct((count, 2, si...  18.3 us
    pallas_call x1, Pallas kernels, restore(): pl.pallas_call(inverse_kernel, out_shape=jax.ShapeDtypeStruct((rows, size...  15.1 us
  transfers between devices with their start and end apart: 9, of which 5 were waited for; matrix products, arithmetic and copies ran while one was open for 0% of the time, Pallas kernels for 17%

profile of v1, /device:TPU:15, one launch (start us, length us, event | category | flops | bytes accessed | tf_op | source)
XLA Modules:
  0.0 527.4 jit_solution(7765655911044231937)
XLA Ops:
  0.0 10.0 %transform.2 = bf16[48,32,512]{2,1,0:T(8,128)(2,1)} custom-call(bf16[32,512,512]{2,1,0:T(8,128)(2,1)} %traces_ref.3, bf16[48,512]{1,0:T(8,128)(2,1)} %constant.12.clone.table_ref), custom_call_target="tpu_custom_call" | custom-call | flops 805306368 | bytes 18350080 | tf_op jit(solution)/shard_map/transform/pallas_call | solution.py:82
  10.0 4.5 all-to-all-start
  14.4 12.8 %transform.3 = (bf16[64,32,512]{2,1,0:T(8,128)(2,1)}, bf16[80,32,512]{2,1,0:T(8,128)(2,1)}, bf16[64,32,512]{2,1,0:T(8,128)(2,1)}) custom-call(bf16[32,512,512]{2,1,0:T(8,128)(2,1)} %traces_ref.3, bf16[208,512]{1,0:T(8,128)(2,1)} %constant.13.clone.table_ref), custom_call_target="tpu_custom_call" | custom-call | flops 3489660928 | bytes 23592960 | tf_op jit(solution)/shard_map/transform/pallas_call | solution.py:82
  27.2 5.2 all-to-all-done.mine_ref
  32.5 30.8 %all_to_all.40.mine_ref = bf16[8,4,2,32,512]{4,3,2,1,0:T(8,128)(2,1)} all-to-all(bf16[8,4,2,32,512]{4,3,2,1,0:T(8,128)(2,1)} %bitcast.14), channel_id=1, replica_groups=mesh['lines'=2,'half'=2,'member'=8] {'member'}, dimensions={0} | all-to-all | bytes 4194304 | tf_op jit(solution)/shard_map/all_to_all | solution.py:256
  63.3 29.2 %all_to_all.41.mine_ref = bf16[8,4,2,32,512]{4,3,2,1,0:T(8,128)(2,1)} all-to-all(bf16[8,4,2,32,512]{4,3,2,1,0:T(8,128)(2,1)S(1)} %bitcast.13), channel_id=1, replica_groups=mesh['lines'=2,'half'=2,'member'=8] {'member'}, dimensions={0} | all-to-all | bytes 4194304 | tf_op jit(solution)/shard_map/all_to_all | solution.py:256
  92.4 5.4 %all-to-all-start.4 = ((bf16[8,5,2,32,512]{4,3,2,1,0:T(8,128)(2,1)}), bf16[8,5,2,32,512]{4,3,2,1,0:T(8,128)(2,1)S(1)}, u32[]{:S(2)}, u32[]{:S(2)}) async-start(bf16[8,5,2,32,512]{4,3,2,1,0:T(8,128)(2,1)} %bitcast.12), calls=%async_computation.4 | async-start | bytes 5242880 | tf_op jit(solution)/shard_map/all_to_all | solution.py:256
  97.9 3.9 pack.4
  104.1 50.9 %collective-permute-done.got_ref = bf16[2320,256]{1,0:T(8,128)(2,1)} collective-permute-done((bf16[2320,256]{1,0:T(8,128)(2,1)}, bf16[2320,256]{1,0:T(8,128)(2,1)}, u32[]{:S(2)}, u32[]{:S(2)}) %collective-permute-start) | collective-permute-done | bytes 1187872 | tf_op jit(solution)/shard_map/ppermute | solution.py:258
  155.0 11.3 %products.4 = bf16[8,3,2,32,512]{4,3,2,1,0:T(8,128)(2,1)} custom-call(s32[1]{0:T(128)} %bitcast.half_ref, bf16[3,2,256,256]{3,2,1,0:T(8,128)(2,1)} %get-tuple-element.16.own_ref, bf16[2320,256]{1,0:T(8,128)(2,1)} %get-tuple-element.17.sent_ref, bf16[2320,256]{1,0:T(8,128)(2,1)} %collective-permute-done.got_ref), custom_call_target="tpu_custom_call" | custom-call | flops 4831838208 | bytes 3932160 | tf_op jit(solution)/shard_map/products/pallas_call | solution.py:224
  166.3 6.2 %all-to-all-start.1 = ((bf16[8,3,2,32,512]{4,3,2,1,0:T(8,128)(2,1)}), bf16[8,3,2,32,512]{4,3,2,1,0:T(8,128)(2,1)}, u32[]{:S(2)}, u32[]{:S(2)}) async-start(bf16[8,3,2,32,512]{4,3,2,1,0:T(8,128)(2,1)} %products.4), calls=%async_computation.1 | async-start | bytes 3145728 | tf_op jit(solution)/shard_map/all_to_all | solution.py:260
  172.5 4.5 pack.5
  178.9 67.7 %collective-permute-done.1.got_ref = bf16[3088,256]{1,0:T(8,128)(2,1)S(1)} collective-permute-done((bf16[3088,256]{1,0:T(8,128)(2,1)}, bf16[3088,256]{1,0:T(8,128)(2,1)S(1)}, u32[]{:S(2)}, u32[]{:S(2)}) %collective-permute-start.1) | collective-permute-done | bytes 1581088 | tf_op jit(solution)/shard_map/ppermute | solution.py:258
  247.8 14.5 %products.5 = bf16[8,4,2,32,512]{4,3,2,1,0:T(8,128)(2,1)} custom-call(s32[1]{0:T(128)} %bitcast.half_ref, bf16[4,2,256,256]{3,2,1,0:T(8,128)(2,1)} %get-tuple-element.19.own_ref, bf16[3088,256]{1,0:T(8,128)(2,1)} %get-tuple-element.20.sent_ref, bf16[3088,256]{1,0:T(8,128)(2,1)} %copy-done.5), custom_call_target="tpu_custom_call" | custom-call | flops 6442450944 | bytes 5242880 | tf_op jit(solution)/shard_map/products/pallas_call | solution.py:224
  262.3 5.9 %all-to-all-start.3 = ((bf16[8,4,2,32,512]{4,3,2,1,0:T(8,128)(2,1)}), bf16[8,4,2,32,512]{4,3,2,1,0:T(8,128)(2,1)S(1)}, u32[]{:S(2)}, u32[]{:S(2)}) async-start(bf16[8,4,2,32,512]{4,3,2,1,0:T(8,128)(2,1)} %products.5), calls=%async_computation.3 | async-start | bytes 4194304 | tf_op jit(solution)/shard_map/all_to_all | solution.py:260
  268.2 4.4 pack.7
  274.9 67.8 %collective-permute-done.3.got_ref = bf16[3088,256]{1,0:T(8,128)(2,1)} collective-permute-done((bf16[3088,256]{1,0:T(8,128)(2,1)}, bf16[3088,256]{1,0:T(8,128)(2,1)}, u32[]{:S(2)}, u32[]{:S(2)}) %collective-permute-start.3) | collective-permute-done | bytes 1581088 | tf_op jit(solution)/shard_map/ppermute | solution.py:258
  342.6 14.5 %products.7 = bf16[8,4,2,32,512]{4,3,2,1,0:T(8,128)(2,1)} custom-call(s32[1]{0:T(128)} %bitcast.half_ref, bf16[4,2,256,256]{3,2,1,0:T(8,128)(2,1)} %get-tuple-element.25.own_ref, bf16[3088,256]{1,0:T(8,128)(2,1)} %get-tuple-element.26.sent_ref, bf16[3088,256]{1,0:T(8,128)(2,1)} %collective-permute-done.3.got_ref), custom_call_target="tpu_custom_call" | custom-call | flops 6442450944 | bytes 5242880 | tf_op jit(solution)/shard_map/products/pallas_call | solution.py:224
  358.4 6.3 %all-to-all-start.7 = ((bf16[8,4,2,32,512]{4,3,2,1,0:T(8,128)(2,1)}), bf16[8,4,2,32,512]{4,3,2,1,0:T(8,128)(2,1)}, u32[]{:S(2)}, u32[]{:S(2)}) async-start(bf16[8,4,2,32,512]{4,3,2,1,0:T(8,128)(2,1)} %products.7), calls=%async_computation.7 | async-start | bytes 4194304 | tf_op jit(solution)/shard_map/all_to_all | solution.py:260
  364.8 5.5 %pack.6 = (bf16[5,2,256,256]{3,2,1,0:T(8,128)(2,1)}, bf16[3856,256]{1,0:T(8,128)(2,1)}) custom-call(s32[1]{0:T(128)} %bitcast.half_ref, bf16[8,5,2,32,512]{4,3,2,1,0:T(8,128)(2,1)} %copy-done), custom_call_target="tpu_custom_call" | custom-call | flops 2621440 | bytes 6553600 | tf_op jit(solution)/shard_map/pack/pallas_call | solution.py:197
  372.1 84.5 %collective-permute-done.2.got_ref = bf16[3856,256]{1,0:T(8,128)(2,1)S(1)} collective-permute-done((bf16[3856,256]{1,0:T(8,128)(2,1)}, bf16[3856,256]{1,0:T(8,128)(2,1)S(1)}, u32[]{:S(2)}, u32[]{:S(2)}) %collective-permute-start.2) | collective-permute-done | bytes 1974304 | tf_op jit(solution)/shard_map/ppermute | solution.py:258
  457.9 17.7 %products.6 = bf16[8,5,2,32,512]{4,3,2,1,0:T(8,128)(2,1)} custom-call(s32[1]{0:T(128)} %bitcast.half_ref, bf16[5,2,256,256]{3,2,1,0:T(8,128)(2,1)} %get-tuple-element.22.own_ref, bf16[3856,256]{1,0:T(8,128)(2,1)} %get-tuple-element.23.sent_ref, bf16[3856,256]{1,0:T(8,128)(2,1)} %copy-done.4), custom_call_target="tpu_custom_call" | custom-call | flops 8053063680 | bytes 6553600 | tf_op jit(solution)/shard_map/products/pallas_call | solution.py:224
  475.5 36.7 %all_to_all.42 = bf16[8,5,2,32,512]{4,3,2,1,0:T(8,128)(2,1)} all-to-all(bf16[8,5,2,32,512]{4,3,2,1,0:T(8,128)(2,1)} %products.6), channel_id=1, replica_groups=mesh['lines'=2,'half'=2,'member'=8] {'member'}, dimensions={0} | all-to-all | bytes 5242880 | tf_op jit(solution)/shard_map/all_to_all | solution.py:260
  512.3 15.1 %restore.1 = bf16[32,512,512]{2,1,0:T(8,128)(2,1)} custom-call(bf16[48,32,512]{2,1,0:T(8,128)(2,1)} %bitcast.2.refs_0_, bf16[64,32,512]{2,1,0:T(8,128)(2,1)} %bitcast.10, bf16[80,32,512]{2,1,0:T(8,128)(2,1)} %bitcast.9, bf16[64,32,512]{2,1,0:T(8,128)(2,1)} %bitcast.8.refs_3_, bf16[256,512]{1,0:T(8,128)(2,1)} %constant.14.clone.refs_4_), custom_call_target="tpu_custom_call" | custom-call | flops 4294967296 | bytes 25165824 | tf_op jit(solution)/shard_map/restore/pallas_call | solution.py:105
  (20 shorter events, 12.1 us)
Async XLA Ops:
  10.0 22.5 %all-to-all-start = ((bf16[8,3,2,32,512]{4,3,2,1,0:T(8,128)(2,1)}), bf16[8,3,2,32,512]{4,3,2,1,0:T(8,128)(2,1)S(1)}, u32[]{:S(2)}, u32[]{:S(2)}) async-start(bf16[8,3,2,32,512]{4,3,2,1,0:T(8,128)(2,1)} %bitcast.11), calls=%async_computation | async-start | bytes 3145728 | tf_op jit(solution)/shard_map/all_to_all | solution.py:256
  32.5 30.8 %copy-start.2 = (bf16[8,3,2,32,512]{4,3,2,1,0:T(8,128)(2,1)}, bf16[8,3,2,32,512]{4,3,2,1,0:T(8,128)(2,1)S(1)}, u32[]{:S(2)}) copy-start(bf16[8,3,2,32,512]{4,3,2,1,0:T(8,128)(2,1)S(1)} %all-to-all-done.mine_ref) | copy-start | bytes 4718596
  32.5 30.8 %copy-start.3 = (bf16[64,32,512]{2,1,0:T(8,128)(2,1)S(1)}, bf16[64,32,512]{2,1,0:T(8,128)(2,1)}, u32[]{:S(2)}) copy-start(bf16[64,32,512]{2,1,0:T(8,128)(2,1)} %get-tuple-element.24) | copy-start | bytes 6291460
  92.4 73.8 %all-to-all-start.4 = ((bf16[8,5,2,32,512]{4,3,2,1,0:T(8,128)(2,1)}), bf16[8,5,2,32,512]{4,3,2,1,0:T(8,128)(2,1)S(1)}, u32[]{:S(2)}, u32[]{:S(2)}) async-start(bf16[8,5,2,32,512]{4,3,2,1,0:T(8,128)(2,1)} %bitcast.12), calls=%async_computation.4 | async-start | bytes 5242880 | tf_op jit(solution)/shard_map/all_to_all | solution.py:256
  101.8 53.2 %collective-permute-start = (bf16[2320,256]{1,0:T(8,128)(2,1)}, bf16[2320,256]{1,0:T(8,128)(2,1)}, u32[]{:S(2)}, u32[]{:S(2)}) collective-permute-start(bf16[2320,256]{1,0:T(8,128)(2,1)} %get-tuple-element.17.sent_ref), channel_id=1, source_target_pairs={{0,8},{8,0},{1,9},{9,1},{2,10},{10,2},{3,11},{11,3},{4,12},{12,4},... | collective-permute-start | bytes 3563528 | tf_op jit(solution)/shard_map/ppermute | solution.py:258
  166.3 10.7 %copy-start = (bf16[8,5,2,32,512]{4,3,2,1,0:T(8,128)(2,1)}, bf16[8,5,2,32,512]{4,3,2,1,0:T(8,128)(2,1)S(1)}, u32[]{:S(2)}) copy-start(bf16[8,5,2,32,512]{4,3,2,1,0:T(8,128)(2,1)S(1)} %all-to-all-done.4.mine_ref) | copy-start | bytes 7864324
  166.3 96.0 %all-to-all-start.1 = ((bf16[8,3,2,32,512]{4,3,2,1,0:T(8,128)(2,1)}), bf16[8,3,2,32,512]{4,3,2,1,0:T(8,128)(2,1)}, u32[]{:S(2)}, u32[]{:S(2)}) async-start(bf16[8,3,2,32,512]{4,3,2,1,0:T(8,128)(2,1)} %products.4), calls=%async_computation.1 | async-start | bytes 3145728 | tf_op jit(solution)/shard_map/all_to_all | solution.py:260
  177.0 69.7 %collective-permute-start.1 = (bf16[3088,256]{1,0:T(8,128)(2,1)}, bf16[3088,256]{1,0:T(8,128)(2,1)S(1)}, u32[]{:S(2)}, u32[]{:S(2)}) collective-permute-start(bf16[3088,256]{1,0:T(8,128)(2,1)} %get-tuple-element.20.sent_ref), channel_id=1, source_target_pairs={{0,8},{8,0},{1,9},{9,1},{2,10},{10,2},{3,11},{11,3},{4,12},{12,4},... | collective-permute-start | bytes 4743176 | tf_op jit(solution)/shard_map/ppermute | solution.py:258
  246.6 1.2 copy-start.5
  262.3 94.8 %all-to-all-start.3 = ((bf16[8,4,2,32,512]{4,3,2,1,0:T(8,128)(2,1)}), bf16[8,4,2,32,512]{4,3,2,1,0:T(8,128)(2,1)S(1)}, u32[]{:S(2)}, u32[]{:S(2)}) async-start(bf16[8,4,2,32,512]{4,3,2,1,0:T(8,128)(2,1)} %products.5), calls=%async_computation.3 | async-start | bytes 4194304 | tf_op jit(solution)/shard_map/all_to_all | solution.py:260
  272.6 70.0 %collective-permute-start.3 = (bf16[3088,256]{1,0:T(8,128)(2,1)}, bf16[3088,256]{1,0:T(8,128)(2,1)}, u32[]{:S(2)}, u32[]{:S(2)}) collective-permute-start(bf16[3088,256]{1,0:T(8,128)(2,1)} %get-tuple-element.26.sent_ref), channel_id=1, source_target_pairs={{0,8},{8,0},{1,9},{9,1},{2,10},{10,2},{3,11},{11,3},{4,12},{12,4},... | collective-permute-start | bytes 4743176 | tf_op jit(solution)/shard_map/ppermute | solution.py:258
  357.1 1.3 copy-start.1
  358.4 117.1 %all-to-all-start.7 = ((bf16[8,4,2,32,512]{4,3,2,1,0:T(8,128)(2,1)}), bf16[8,4,2,32,512]{4,3,2,1,0:T(8,128)(2,1)}, u32[]{:S(2)}, u32[]{:S(2)}) async-start(bf16[8,4,2,32,512]{4,3,2,1,0:T(8,128)(2,1)} %products.7), calls=%async_computation.7 | async-start | bytes 4194304 | tf_op jit(solution)/shard_map/all_to_all | solution.py:260
  370.2 86.4 %collective-permute-start.2 = (bf16[3856,256]{1,0:T(8,128)(2,1)}, bf16[3856,256]{1,0:T(8,128)(2,1)S(1)}, u32[]{:S(2)}, u32[]{:S(2)}) collective-permute-start(bf16[3856,256]{1,0:T(8,128)(2,1)} %get-tuple-element.23.sent_ref), channel_id=1, source_target_pairs={{0,8},{8,0},{1,9},{9,1},{2,10},{10,2},{3,11},{11,3},{4,12},{12,4},... | collective-permute-start | bytes 5922824 | tf_op jit(solution)/shard_map/ppermute | solution.py:258
  456.6 1.3 copy-start.4

commit v2 on v1

--- a/solution.py
+++ b/solution.py
@@ -143,7 +143,7 @@
     sent_ref[tail:] = jnp.where(line == step, diagonal, before).astype(jnp.bfloat16)
 
 
-def product_kernel(half_ref, own_ref, sent_ref, got_ref, out_ref, lhs_ref, rhs_ref, sum_ref):
+def product_kernel(half_ref, own_ref, sent_ref, got_ref, tail_ref, out_ref, lhs_ref, rhs_ref, sum_ref):
     group, rows, full = out_ref.shape[0], out_ref.shape[3], out_ref.shape[4]
     size = full // 2
     eta = 1.0 / math.sqrt(full)
@@ -152,10 +152,9 @@
     far = pl.multiple_of((1 - half) * size, size)
     row, col = grid_masks(size)
     step = pl.program_id(0)
-    start = step * (3 * size)
-    packed = got_ref[pl.ds(pl.multiple_of(start + 2 * size, size), size)].astype(jnp.float32)
+    packed = got_ref[2 * size : 3 * size].astype(jnp.float32)
     turned = packed.T
-    tail = got_ref[got_ref.shape[0] - TAIL :].astype(jnp.float32)
+    tail = tail_ref[...].astype(jnp.float32)
     line = lax.broadcasted_iota(jnp.int32, (TAIL, size), 0)
     diagonal = jnp.sum(jnp.where(line == step, tail, 0.0), axis=0, keepdims=True)
     there = (
@@ -163,7 +162,7 @@
         jnp.where(row > col, packed, jnp.where(row < col, turned, diagonal)),
     )
     for c in range(2):
-        at = pl.ds(pl.multiple_of(start + c * size, size), size)
+        at = slice(c * size, (c + 1) * size)
         mixed = (sent_ref[at].astype(jnp.float32) + got_ref[at].astype(jnp.float32).T) * 0.5
         mixed = mixed.astype(jnp.bfloat16)
         turned = mixed.astype(jnp.float32).T.astype(jnp.bfloat16)
@@ -220,14 +219,15 @@
     full = 2 * size
     rows = size // group
     shape = jax.ShapeDtypeStruct((group, count, 2, rows, full), jnp.bfloat16)
-    passed = pl.BlockSpec(got.shape, lambda k, h: (0, 0))
+    passed = pl.BlockSpec((3 * size, size), lambda k, h: (k, 0))
+    last = pl.BlockSpec((TAIL, size), lambda k, h: (count * 3 * size // TAIL, 0))
     return pl.pallas_call(
         product_kernel,
         out_shape=shape,
         grid_spec=pltpu.PrefetchScalarGridSpec(
             num_scalar_prefetch=1,
             grid=(count,),
-            in_specs=[pl.BlockSpec((1, 2, size, size), lambda k, h: (k, 0, 0, 0)), passed, passed],
+            in_specs=[pl.BlockSpec((1, 2, size, size), lambda k, h: (k, 0, 0, 0)), passed, passed, last],
             out_specs=pl.BlockSpec((group, 1, 2, rows, full), lambda k, h: (0, k, 0, 0, 0)),
             scratch_shapes=[
                 pltpu.VMEM((2 * full, 2 * full), jnp.bfloat16),
@@ -238,7 +238,7 @@
         compiler_params=pltpu.CompilerParams(vmem_limit_bytes=VMEM),
         cost_estimate=pl.CostEstimate(flops=count * full**3 * 12, bytes_accessed=count * full * full * 5, transcendentals=0),
         name="products",
-    )(half, own, sent, got)
+    )(half, own, sent, got, got)
 
 
 def local(group, traces):

time: 531 us -> 528 us (level)
  transfers between devices with their start and end apart: 9 -> 9, of which waited for: 5 -> 5; matrix products, arithmetic and copies ran while one was open for 0% -> 0% of each run, Pallas kernels for 17% -> 16%
where the time goes in v2:
time: 528 us; the launch traced here: 524 us
  waiting for transfers between devices  276 us (52%)
  Pallas kernels  111 us (21%)
  blocking collectives  96.7 us (18%)
  starting transfers between devices  36.7 us (7%)
    ppermute x4, waiting for transfers between devices, local(): got = lax.ppermute(sent, 'half', [(0, 1), (1, 0)])  271 us
    all_to_all x2, blocking collectives, local(): lax.all_to_all(spectrum, 'member', split_axis=0, concat_axis=0, tiled=True)  59.9 us
    pallas_call x4, Pallas kernels, products(): pl.pallas_call(product_kernel, out_shape=shape, grid_spec=pltpu.PrefetchS...  54.8 us
    all_to_all x1, blocking collectives, local(): lax.all_to_all(predicted, 'member', split_axis=0, concat_axis=0, tiled=True)  36.7 us
    pallas_call x2, Pallas kernels, transform(): pl.pallas_call(forward_kernel, out_shape=tuple((jax.ShapeDtypeStruct((n,...  22.8 us
    all_to_all x3, starting transfers between devices, local(): lax.all_to_all(predicted, 'member', split_axis=0, concat_axis=0, tiled=True)  18.4 us
    pallas_call x4, Pallas kernels, pack(): pl.pallas_call(pack_kernel, out_shape=(jax.ShapeDtypeStruct((count, 2, si...  18.3 us
    pallas_call x1, Pallas kernels, restore(): pl.pallas_call(inverse_kernel, out_shape=jax.ShapeDtypeStruct((rows, size...  15.1 us
  transfers between devices with their start and end apart: 9, of which 5 were waited for; matrix products, arithmetic and copies ran while one was open for 0% of the time, Pallas kernels for 16%

profile of v2, /device:TPU:15, one launch (start us, length us, event | category | flops | bytes accessed | tf_op | source)
XLA Modules:
  0.0 524.3 jit_solution(18115201058447287234)
XLA Ops:
  0.0 10.0 %transform.2 = bf16[48,32,512]{2,1,0:T(8,128)(2,1)} custom-call(bf16[32,512,512]{2,1,0:T(8,128)(2,1)} %traces_ref.3, bf16[48,512]{1,0:T(8,128)(2,1)} %constant.12.clone.table_ref), custom_call_target="tpu_custom_call" | custom-call | flops 805306368 | bytes 18350080 | tf_op jit(solution)/shard_map/transform/pallas_call | solution.py:82
  10.0 4.5 all-to-all-start
  14.4 12.8 %transform.3 = (bf16[64,32,512]{2,1,0:T(8,128)(2,1)}, bf16[80,32,512]{2,1,0:T(8,128)(2,1)}, bf16[64,32,512]{2,1,0:T(8,128)(2,1)}) custom-call(bf16[32,512,512]{2,1,0:T(8,128)(2,1)} %traces_ref.3, bf16[208,512]{1,0:T(8,128)(2,1)} %constant.13.clone.table_ref), custom_call_target="tpu_custom_call" | custom-call | flops 3489660928 | bytes 23592960 | tf_op jit(solution)/shard_map/transform/pallas_call | solution.py:82
  27.2 5.2 %all-to-all-done.mine_ref = bf16[8,3,2,32,512]{4,3,2,1,0:T(8,128)(2,1)S(1)} async-done(((bf16[8,3,2,32,512]{4,3,2,1,0:T(8,128)(2,1)}), bf16[8,3,2,32,512]{4,3,2,1,0:T(8,128)(2,1)S(1)}, u32[]{:S(2)}, u32[]{:S(2)}) %all-to-all-start) | async-done | bytes 1572896 | tf_op jit(solution)/shard_map/all_to_all | solution.py:256
  32.5 30.8 %all_to_all.40.mine_ref = bf16[8,4,2,32,512]{4,3,2,1,0:T(8,128)(2,1)} all-to-all(bf16[8,4,2,32,512]{4,3,2,1,0:T(8,128)(2,1)} %bitcast.14), channel_id=1, replica_groups=mesh['lines'=2,'half'=2,'member'=8] {'member'}, dimensions={0} | all-to-all | bytes 4194304 | tf_op jit(solution)/shard_map/all_to_all | solution.py:256
  63.3 29.2 %all_to_all.41.mine_ref = bf16[8,4,2,32,512]{4,3,2,1,0:T(8,128)(2,1)} all-to-all(bf16[8,4,2,32,512]{4,3,2,1,0:T(8,128)(2,1)S(1)} %bitcast.13), channel_id=1, replica_groups=mesh['lines'=2,'half'=2,'member'=8] {'member'}, dimensions={0} | all-to-all | bytes 4194304 | tf_op jit(solution)/shard_map/all_to_all | solution.py:256
  92.4 5.4 %all-to-all-start.4 = ((bf16[8,5,2,32,512]{4,3,2,1,0:T(8,128)(2,1)}), bf16[8,5,2,32,512]{4,3,2,1,0:T(8,128)(2,1)S(1)}, u32[]{:S(2)}, u32[]{:S(2)}) async-start(bf16[8,5,2,32,512]{4,3,2,1,0:T(8,128)(2,1)} %bitcast.12), calls=%async_computation.4 | async-start | bytes 5242880 | tf_op jit(solution)/shard_map/all_to_all | solution.py:256
  97.9 3.9 pack.4
  104.1 50.9 %collective-permute-done.got_ref.tail_ref = bf16[2320,256]{1,0:T(8,128)(2,1)} collective-permute-done((bf16[2320,256]{1,0:T(8,128)(2,1)}, bf16[2320,256]{1,0:T(8,128)(2,1)}, u32[]{:S(2)}, u32[]{:S(2)}) %collective-permute-start) | collective-permute-done | bytes 1187872 | tf_op jit(solution)/shard_map/ppermute | solution.py:258
  155.0 10.8 %products.4 = bf16[8,3,2,32,512]{4,3,2,1,0:T(8,128)(2,1)} custom-call(s32[1]{0:T(128)} %bitcast.half_ref, bf16[3,2,256,256]{3,2,1,0:T(8,128)(2,1)} %get-tuple-element.16.own_ref, bf16[2320,256]{1,0:T(8,128)(2,1)} %get-tuple-element.17.sent_ref, bf16[2320,256]{1,0:T(8,128)(2,1)} %collective-permute-done.got_ref.tail_ref, ...), custom_call_target="tpu_custom_call" | custom-call | flops 4831838208 | bytes 3932160 | tf_op jit(solution)/shard_map/products/pallas_call | solution.py:224
  165.8 6.2 %all-to-all-start.1 = ((bf16[8,3,2,32,512]{4,3,2,1,0:T(8,128)(2,1)}), bf16[8,3,2,32,512]{4,3,2,1,0:T(8,128)(2,1)}, u32[]{:S(2)}, u32[]{:S(2)}) async-start(bf16[8,3,2,32,512]{4,3,2,1,0:T(8,128)(2,1)} %products.4), calls=%async_computation.1 | async-start | bytes 3145728 | tf_op jit(solution)/shard_map/all_to_all | solution.py:260
  172.0 4.5 pack.5
  178.4 67.7 %collective-permute-done.1.got_ref.tail_ref = bf16[3088,256]{1,0:T(8,128)(2,1)S(1)} collective-permute-done((bf16[3088,256]{1,0:T(8,128)(2,1)}, bf16[3088,256]{1,0:T(8,128)(2,1)S(1)}, u32[]{:S(2)}, u32[]{:S(2)}) %collective-permute-start.1) | collective-permute-done | bytes 1581088 | tf_op jit(solution)/shard_map/ppermute | solution.py:258
  247.3 13.7 %products.5 = bf16[8,4,2,32,512]{4,3,2,1,0:T(8,128)(2,1)} custom-call(s32[1]{0:T(128)} %bitcast.half_ref, bf16[4,2,256,256]{3,2,1,0:T(8,128)(2,1)} %get-tuple-element.19.own_ref, bf16[3088,256]{1,0:T(8,128)(2,1)} %get-tuple-element.20.sent_ref, bf16[3088,256]{1,0:T(8,128)(2,1)} %copy-done.5, bf16[3088,256]{1,0:T(8,128)(2,1)} %copy-done.5), custom_call_target="tpu_custom_call" | custom-call | flops 6442450944 | bytes 5242880 | tf_op jit(solution)/shard_map/products/pallas_call | solution.py:224
  261.0 5.9 %all-to-all-start.3 = ((bf16[8,4,2,32,512]{4,3,2,1,0:T(8,128)(2,1)}), bf16[8,4,2,32,512]{4,3,2,1,0:T(8,128)(2,1)S(1)}, u32[]{:S(2)}, u32[]{:S(2)}) async-start(bf16[8,4,2,32,512]{4,3,2,1,0:T(8,128)(2,1)} %products.5), calls=%async_computation.3 | async-start | bytes 4194304 | tf_op jit(solution)/shard_map/all_to_all | solution.py:260
  266.9 4.4 pack.7
  273.6 67.8 %collective-permute-done.3.got_ref.tail_ref = bf16[3088,256]{1,0:T(8,128)(2,1)} collective-permute-done((bf16[3088,256]{1,0:T(8,128)(2,1)}, bf16[3088,256]{1,0:T(8,128)(2,1)}, u32[]{:S(2)}, u32[]{:S(2)}) %collective-permute-start.3) | collective-permute-done | bytes 1581088 | tf_op jit(solution)/shard_map/ppermute | solution.py:258
  341.4 13.7 %products.7 = bf16[8,4,2,32,512]{4,3,2,1,0:T(8,128)(2,1)} custom-call(s32[1]{0:T(128)} %bitcast.half_ref, bf16[4,2,256,256]{3,2,1,0:T(8,128)(2,1)} %get-tuple-element.25.own_ref, bf16[3088,256]{1,0:T(8,128)(2,1)} %get-tuple-element.26.sent_ref, bf16[3088,256]{1,0:T(8,128)(2,1)} %collective-permute-done.3.got_ref.tail_ref, ...), custom_call_target="tpu_custom_call" | custom-call | flops 6442450944 | bytes 5242880 | tf_op jit(solution)/shard_map/products/pallas_call | solution.py:224
  356.4 6.3 %all-to-all-start.7 = ((bf16[8,4,2,32,512]{4,3,2,1,0:T(8,128)(2,1)}), bf16[8,4,2,32,512]{4,3,2,1,0:T(8,128)(2,1)}, u32[]{:S(2)}, u32[]{:S(2)}) async-start(bf16[8,4,2,32,512]{4,3,2,1,0:T(8,128)(2,1)} %products.7), calls=%async_computation.7 | async-start | bytes 4194304 | tf_op jit(solution)/shard_map/all_to_all | solution.py:260
  362.7 5.5 %pack.6 = (bf16[5,2,256,256]{3,2,1,0:T(8,128)(2,1)}, bf16[3856,256]{1,0:T(8,128)(2,1)}) custom-call(s32[1]{0:T(128)} %bitcast.half_ref, bf16[8,5,2,32,512]{4,3,2,1,0:T(8,128)(2,1)} %copy-done), custom_call_target="tpu_custom_call" | custom-call | flops 2621440 | bytes 6553600 | tf_op jit(solution)/shard_map/pack/pallas_call | solution.py:196
  370.0 84.5 %collective-permute-done.2.got_ref.tail_ref = bf16[3856,256]{1,0:T(8,128)(2,1)S(1)} collective-permute-done((bf16[3856,256]{1,0:T(8,128)(2,1)}, bf16[3856,256]{1,0:T(8,128)(2,1)S(1)}, u32[]{:S(2)}, u32[]{:S(2)}) %collective-permute-start.2) | collective-permute-done | bytes 1974304 | tf_op jit(solution)/shard_map/ppermute | solution.py:258
  455.8 16.6 %products.6 = bf16[8,5,2,32,512]{4,3,2,1,0:T(8,128)(2,1)} custom-call(s32[1]{0:T(128)} %bitcast.half_ref, bf16[5,2,256,256]{3,2,1,0:T(8,128)(2,1)} %get-tuple-element.22.own_ref, bf16[3856,256]{1,0:T(8,128)(2,1)} %get-tuple-element.23.sent_ref, bf16[3856,256]{1,0:T(8,128)(2,1)} %copy-done.4, bf16[3856,256]{1,0:T(8,128)(2,1)} %copy-done.4), custom_call_target="tpu_custom_call" | custom-call | flops 8053063680 | bytes 6553600 | tf_op jit(solution)/shard_map/products/pallas_call | solution.py:224
  472.5 36.7 %all_to_all.42 = bf16[8,5,2,32,512]{4,3,2,1,0:T(8,128)(2,1)} all-to-all(bf16[8,5,2,32,512]{4,3,2,1,0:T(8,128)(2,1)} %products.6), channel_id=1, replica_groups=mesh['lines'=2,'half'=2,'member'=8] {'member'}, dimensions={0} | all-to-all | bytes 5242880 | tf_op jit(solution)/shard_map/all_to_all | solution.py:260
  509.2 15.1 %restore.1 = bf16[32,512,512]{2,1,0:T(8,128)(2,1)} custom-call(bf16[48,32,512]{2,1,0:T(8,128)(2,1)} %bitcast.2.refs_0_, bf16[64,32,512]{2,1,0:T(8,128)(2,1)} %bitcast.10, bf16[80,32,512]{2,1,0:T(8,128)(2,1)} %bitcast.9, bf16[64,32,512]{2,1,0:T(8,128)(2,1)} %bitcast.8.refs_3_, bf16[256,512]{1,0:T(8,128)(2,1)} %constant.14.clone.refs_4_), custom_call_target="tpu_custom_call" | custom-call | flops 4294967296 | bytes 25165824 | tf_op jit(solution)/shard_map/restore/pallas_call | solution.py:105
  (20 shorter events, 12.1 us)
Async XLA Ops:
  10.0 22.5 %all-to-all-start = ((bf16[8,3,2,32,512]{4,3,2,1,0:T(8,128)(2,1)}), bf16[8,3,2,32,512]{4,3,2,1,0:T(8,128)(2,1)S(1)}, u32[]{:S(2)}, u32[]{:S(2)}) async-start(bf16[8,3,2,32,512]{4,3,2,1,0:T(8,128)(2,1)} %bitcast.11), calls=%async_computation | async-start | bytes 3145728 | tf_op jit(solution)/shard_map/all_to_all | solution.py:256
  32.5 30.8 %copy-start.2 = (bf16[8,3,2,32,512]{4,3,2,1,0:T(8,128)(2,1)}, bf16[8,3,2,32,512]{4,3,2,1,0:T(8,128)(2,1)S(1)}, u32[]{:S(2)}) copy-start(bf16[8,3,2,32,512]{4,3,2,1,0:T(8,128)(2,1)S(1)} %all-to-all-done.mine_ref) | copy-start | bytes 4718596
  32.5 30.8 %copy-start.3 = (bf16[64,32,512]{2,1,0:T(8,128)(2,1)S(1)}, bf16[64,32,512]{2,1,0:T(8,128)(2,1)}, u32[]{:S(2)}) copy-start(bf16[64,32,512]{2,1,0:T(8,128)(2,1)} %get-tuple-element.24) | copy-start | bytes 6291460
  92.4 73.3 %all-to-all-start.4 = ((bf16[8,5,2,32,512]{4,3,2,1,0:T(8,128)(2,1)}), bf16[8,5,2,32,512]{4,3,2,1,0:T(8,128)(2,1)S(1)}, u32[]{:S(2)}, u32[]{:S(2)}) async-start(bf16[8,5,2,32,512]{4,3,2,1,0:T(8,128)(2,1)} %bitcast.12), calls=%async_computation.4 | async-start | bytes 5242880 | tf_op jit(solution)/shard_map/all_to_all | solution.py:256
  101.8 53.2 %collective-permute-start = (bf16[2320,256]{1,0:T(8,128)(2,1)}, bf16[2320,256]{1,0:T(8,128)(2,1)}, u32[]{:S(2)}, u32[]{:S(2)}) collective-permute-start(bf16[2320,256]{1,0:T(8,128)(2,1)} %get-tuple-element.17.sent_ref), channel_id=1, source_target_pairs={{0,8},{8,0},{1,9},{9,1},{2,10},{10,2},{3,11},{11,3},{4,12},{12,4},... | collective-permute-start | bytes 3563528 | tf_op jit(solution)/shard_map/ppermute | solution.py:258
  165.8 10.7 %copy-start = (bf16[8,5,2,32,512]{4,3,2,1,0:T(8,128)(2,1)}, bf16[8,5,2,32,512]{4,3,2,1,0:T(8,128)(2,1)S(1)}, u32[]{:S(2)}) copy-start(bf16[8,5,2,32,512]{4,3,2,1,0:T(8,128)(2,1)S(1)} %all-to-all-done.4.mine_ref) | copy-start | bytes 7864324
  165.8 95.2 %all-to-all-start.1 = ((bf16[8,3,2,32,512]{4,3,2,1,0:T(8,128)(2,1)}), bf16[8,3,2,32,512]{4,3,2,1,0:T(8,128)(2,1)}, u32[]{:S(2)}, u32[]{:S(2)}) async-start(bf16[8,3,2,32,512]{4,3,2,1,0:T(8,128)(2,1)} %products.4), calls=%async_computation.1 | async-start | bytes 3145728 | tf_op jit(solution)/shard_map/all_to_all | solution.py:260
  176.5 69.7 %collective-permute-start.1 = (bf16[3088,256]{1,0:T(8,128)(2,1)}, bf16[3088,256]{1,0:T(8,128)(2,1)S(1)}, u32[]{:S(2)}, u32[]{:S(2)}) collective-permute-start(bf16[3088,256]{1,0:T(8,128)(2,1)} %get-tuple-element.20.sent_ref), channel_id=1, source_target_pairs={{0,8},{8,0},{1,9},{9,1},{2,10},{10,2},{3,11},{11,3},{4,12},{12,4},... | collective-permute-start | bytes 4743176 | tf_op jit(solution)/shard_map/ppermute | solution.py:258
  246.1 1.2 copy-start.5
  261.0 94.0 %all-to-all-start.3 = ((bf16[8,4,2,32,512]{4,3,2,1,0:T(8,128)(2,1)}), bf16[8,4,2,32,512]{4,3,2,1,0:T(8,128)(2,1)S(1)}, u32[]{:S(2)}, u32[]{:S(2)}) async-start(bf16[8,4,2,32,512]{4,3,2,1,0:T(8,128)(2,1)} %products.5), calls=%async_computation.3 | async-start | bytes 4194304 | tf_op jit(solution)/shard_map/all_to_all | solution.py:260
  271.3 70.0 %collective-permute-start.3 = (bf16[3088,256]{1,0:T(8,128)(2,1)}, bf16[3088,256]{1,0:T(8,128)(2,1)}, u32[]{:S(2)}, u32[]{:S(2)}) collective-permute-start(bf16[3088,256]{1,0:T(8,128)(2,1)} %get-tuple-element.26.sent_ref), channel_id=1, source_target_pairs={{0,8},{8,0},{1,9},{9,1},{2,10},{10,2},{3,11},{11,3},{4,12},{12,4},... | collective-permute-start | bytes 4743176 | tf_op jit(solution)/shard_map/ppermute | solution.py:258
  355.1 1.3 copy-start.1
  356.4 116.1 %all-to-all-start.7 = ((bf16[8,4,2,32,512]{4,3,2,1,0:T(8,128)(2,1)}), bf16[8,4,2,32,512]{4,3,2,1,0:T(8,128)(2,1)}, u32[]{:S(2)}, u32[]{:S(2)}) async-start(bf16[8,4,2,32,512]{4,3,2,1,0:T(8,128)(2,1)} %products.7), calls=%async_computation.7 | async-start | bytes 4194304 | tf_op jit(solution)/shard_map/all_to_all | solution.py:260
  368.2 86.4 %collective-permute-start.2 = (bf16[3856,256]{1,0:T(8,128)(2,1)}, bf16[3856,256]{1,0:T(8,128)(2,1)S(1)}, u32[]{:S(2)}, u32[]{:S(2)}) collective-permute-start(bf16[3856,256]{1,0:T(8,128)(2,1)} %get-tuple-element.23.sent_ref), channel_id=1, source_target_pairs={{0,8},{8,0},{1,9},{9,1},{2,10},{10,2},{3,11},{11,3},{4,12},{12,4},... | collective-permute-start | bytes 5922824 | tf_op jit(solution)/shard_map/ppermute | solution.py:258
  454.6 1.3 copy-start.4

commit v3 on v0

--- a/solution.py
+++ b/solution.py
@@ -11,6 +11,7 @@
 
 F = 128
 VMEM = 60 << 20
+SIZES = (3, 4, 5, 4, 16)
 
 
 def make_tables(nt):
@@ -26,8 +27,8 @@
 
 def split(group):
     share = F // group
-    chunks = math.gcd(4, share)
-    return [share // chunks] * chunks
+    marks = [round(share * mark / SIZES[-1]) for mark in np.cumsum((0,) + SIZES[:-1])]
+    return [b - a for a, b in zip(marks, marks[1:]) if b > a]
 
 
 def grid_masks(size):
@@ -67,12 +68,9 @@
             scratch[lane, at * rows : (at + n) * rows, :] = piece.reshape(n * rows, 128)
         at += n
     for s in range(rows):
-        for lane in range(scratch.shape[0]):
-            value = scratch[lane, pl.ds(s, count, stride=rows), :]
-            value = lax.dot_general(
-                value.T.astype(jnp.bfloat16), table_ref[...], (((1,), (0,)), ((), ())), preferred_element_type=jnp.float32
-            )
-            out_ref[s, lane * 128 : (lane + 1) * 128, :] = value.astype(jnp.bfloat16)
+        lanes = [scratch[lane, pl.ds(s, count, stride=rows), :] for lane in range(scratch.shape[0])]
+        value = jnp.concatenate(lanes, axis=1).T.astype(jnp.bfloat16)
+        out_ref[s] = jnp.dot(value, table_ref[...], preferred_element_type=jnp.float32).astype(jnp.bfloat16)
 
 
 def transform(traces, table, counts):
@@ -238,7 +236,9 @@
     chunks = split(group)
     forward, inverse = make_tables(nt)
     table = forward.reshape(nt, 2 * F).T
-    spectra = transform(traces, jnp.asarray(table), [2 * group * n for n in chunks])
+    counts = [2 * group * n for n in chunks]
+    spectra = transform(traces, jnp.asarray(table[: counts[0]]), counts[:1])
+    spectra += transform(traces, jnp.asarray(table[counts[0] :]), counts[1:])
     parts = []
     for n, spectrum in zip(chunks, spectra):
         spectrum = spectrum.reshape(group, n, 2, rows, size)

time: 535 us -> 532 us (level)
  blocking collectives: 118 us -> 96.7 us
  Pallas kernels: 102 us -> 110 us
    all_to_all x3 -> x2, blocking collectives: 87.8 us -> 59.9 us  [local(): lax.all_to_all(spectrum, 'member', split_axis=0, concat_axis=0, tiled=True)]
    pallas_call x1 -> x2, Pallas kernels: 13.4 us -> 22.8 us  [transform(): pl.pallas_call(forward_kernel, out_shape=tuple((jax.ShapeDtypeStruct((n,...]
    all_to_all x1, blocking collectives: 30.6 us -> 36.7 us  [local(): lax.all_to_all(predicted, 'member', split_axis=0, concat_axis=0, tiled=True)]
  transfers between devices with their start and end apart: 8 -> 9, of which waited for: 4 -> 5; matrix products, arithmetic and copies ran while one was open for 0% -> 0% of each run, Pallas kernels for 13% -> 16%
where the time goes in v3:
time: 532 us; the launch traced here: 528 us
  waiting for transfers between devices  280 us (53%)
  Pallas kernels  110 us (21%)
  blocking collectives  96.7 us (18%)
  starting transfers between devices  36.6 us (7%)
    ppermute x4, waiting for transfers between devices, local(): got = lax.ppermute(sent, 'half', [(0, 1), (1, 0)])  275 us
    all_to_all x2, blocking collectives, local(): lax.all_to_all(spectrum, 'member', split_axis=0, concat_axis=0, tiled=True)  59.9 us
    pallas_call x4, Pallas kernels, products(): pl.pallas_call(product_kernel, out_shape=shape, grid_spec=pltpu.PrefetchS...  54.8 us
    all_to_all x1, blocking collectives, local(): lax.all_to_all(predicted, 'member', split_axis=0, concat_axis=0, tiled=True)  36.7 us
    pallas_call x2, Pallas kernels, transform(): pl.pallas_call(forward_kernel, out_shape=tuple((jax.ShapeDtypeStruct((n,...  22.8 us
    all_to_all x3, starting transfers between devices, local(): lax.all_to_all(predicted, 'member', split_axis=0, concat_axis=0, tiled=True)  18.4 us
    pallas_call x4, Pallas kernels, pack(): pl.pallas_call(pack_kernel, out_shape=(jax.ShapeDtypeStruct((count, 2, si...  17.4 us
    pallas_call x1, Pallas kernels, restore(): pl.pallas_call(inverse_kernel, out_shape=jax.ShapeDtypeStruct((rows, size...  15.1 us
  transfers between devices with their start and end apart: 9, of which 5 were waited for; matrix products, arithmetic and copies ran while one was open for 0% of the time, Pallas kernels for 16%

profile of v3, /device:TPU:15, one launch (start us, length us, event | category | flops | bytes accessed | tf_op | source)
XLA Modules:
  0.0 527.6 jit_solution(10507635811930009708)
XLA Ops:
  0.0 10.0 %transform.2 = bf16[48,32,512]{2,1,0:T(8,128)(2,1)} custom-call(bf16[32,512,512]{2,1,0:T(8,128)(2,1)} %traces_ref.3, bf16[48,512]{1,0:T(8,128)(2,1)} %constant.12.clone.table_ref), custom_call_target="tpu_custom_call" | custom-call | flops 805306368 | bytes 18350080 | tf_op jit(solution)/shard_map/transform/pallas_call | solution.py:81
  10.0 4.5 all-to-all-start
  14.4 12.8 %transform.3 = (bf16[64,32,512]{2,1,0:T(8,128)(2,1)}, bf16[80,32,512]{2,1,0:T(8,128)(2,1)}, bf16[64,32,512]{2,1,0:T(8,128)(2,1)}) custom-call(bf16[32,512,512]{2,1,0:T(8,128)(2,1)} %traces_ref.3, bf16[208,512]{1,0:T(8,128)(2,1)} %constant.13.clone.table_ref), custom_call_target="tpu_custom_call" | custom-call | flops 3489660928 | bytes 23592960 | tf_op jit(solution)/shard_map/transform/pallas_call | solution.py:81
  27.2 5.2 all-to-all-done.mine_ref
  32.5 30.8 %all_to_all.40.mine_ref = bf16[8,4,2,32,512]{4,3,2,1,0:T(8,128)(2,1)} all-to-all(bf16[8,4,2,32,512]{4,3,2,1,0:T(8,128)(2,1)} %bitcast.14), channel_id=1, replica_groups=mesh['lines'=2,'half'=2,'member'=8] {'member'}, dimensions={0} | all-to-all | bytes 4194304 | tf_op jit(solution)/shard_map/all_to_all | solution.py:245
  63.3 29.2 %all_to_all.41.mine_ref = bf16[8,4,2,32,512]{4,3,2,1,0:T(8,128)(2,1)} all-to-all(bf16[8,4,2,32,512]{4,3,2,1,0:T(8,128)(2,1)S(1)} %bitcast.13), channel_id=1, replica_groups=mesh['lines'=2,'half'=2,'member'=8] {'member'}, dimensions={0} | all-to-all | bytes 4194304 | tf_op jit(solution)/shard_map/all_to_all | solution.py:245
  92.4 5.4 %all-to-all-start.4 = ((bf16[8,5,2,32,512]{4,3,2,1,0:T(8,128)(2,1)}), bf16[8,5,2,32,512]{4,3,2,1,0:T(8,128)(2,1)S(1)}, u32[]{:S(2)}, u32[]{:S(2)}) async-start(bf16[8,5,2,32,512]{4,3,2,1,0:T(8,128)(2,1)} %bitcast.12), calls=%async_computation.4 | async-start | bytes 5242880 | tf_op jit(solution)/shard_map/all_to_all | solution.py:245
  97.9 3.8 pack.4
  103.9 51.6 %collective-permute-done.got_ref = bf16[3,784,256]{2,1,0:T(8,128)(2,1)} collective-permute-done((bf16[3,784,256]{2,1,0:T(8,128)(2,1)}, bf16[3,784,256]{2,1,0:T(8,128)(2,1)}, u32[]{:S(2)}, u32[]{:S(2)}) %collective-permute-start) | collective-permute-done | bytes 1204256 | tf_op jit(solution)/shard_map/ppermute | solution.py:247
  155.6 10.8 %products.4 = bf16[8,3,2,32,512]{4,3,2,1,0:T(8,128)(2,1)} custom-call(s32[1]{0:T(128)} %bitcast.half_ref, bf16[3,2,256,256]{3,2,1,0:T(8,128)(2,1)} %get-tuple-element.16.own_ref, bf16[3,784,256]{2,1,0:T(8,128)(2,1)} %get-tuple-element.17.sent_ref, bf16[3,784,256]{2,1,0:T(8,128)(2,1)} %collective-permute-done.got_ref), custom_call_target="tpu_custom_call" | custom-call | flops 4831838208 | bytes 3932160 | tf_op jit(solution)/shard_map/products/pallas_call | solution.py:213
  166.4 6.2 %all-to-all-start.1 = ((bf16[8,3,2,32,512]{4,3,2,1,0:T(8,128)(2,1)}), bf16[8,3,2,32,512]{4,3,2,1,0:T(8,128)(2,1)}, u32[]{:S(2)}, u32[]{:S(2)}) async-start(bf16[8,3,2,32,512]{4,3,2,1,0:T(8,128)(2,1)} %products.4), calls=%async_computation.1 | async-start | bytes 3145728 | tf_op jit(solution)/shard_map/all_to_all | solution.py:249
  172.6 4.2 pack.5
  178.7 68.8 %collective-permute-done.1.got_ref = bf16[4,784,256]{2,1,0:T(8,128)(2,1)S(1)} collective-permute-done((bf16[4,784,256]{2,1,0:T(8,128)(2,1)}, bf16[4,784,256]{2,1,0:T(8,128)(2,1)S(1)}, u32[]{:S(2)}, u32[]{:S(2)}) %collective-permute-start.1) | collective-permute-done | bytes 1605664 | tf_op jit(solution)/shard_map/ppermute | solution.py:247
  248.7 13.7 %products.5 = bf16[8,4,2,32,512]{4,3,2,1,0:T(8,128)(2,1)} custom-call(s32[1]{0:T(128)} %bitcast.half_ref, bf16[4,2,256,256]{3,2,1,0:T(8,128)(2,1)} %get-tuple-element.19.own_ref, bf16[4,784,256]{2,1,0:T(8,128)(2,1)} %get-tuple-element.20.sent_ref, bf16[4,784,256]{2,1,0:T(8,128)(2,1)} %copy-done.5), custom_call_target="tpu_custom_call" | custom-call | flops 6442450944 | bytes 5242880 | tf_op jit(solution)/shard_map/products/pallas_call | solution.py:213
  262.4 5.9 %all-to-all-start.3 = ((bf16[8,4,2,32,512]{4,3,2,1,0:T(8,128)(2,1)}), bf16[8,4,2,32,512]{4,3,2,1,0:T(8,128)(2,1)S(1)}, u32[]{:S(2)}, u32[]{:S(2)}) async-start(bf16[8,4,2,32,512]{4,3,2,1,0:T(8,128)(2,1)} %products.5), calls=%async_computation.3 | async-start | bytes 4194304 | tf_op jit(solution)/shard_map/all_to_all | solution.py:249
  268.3 4.2 pack.7
  274.7 68.8 %collective-permute-done.3.got_ref = bf16[4,784,256]{2,1,0:T(8,128)(2,1)} collective-permute-done((bf16[4,784,256]{2,1,0:T(8,128)(2,1)}, bf16[4,784,256]{2,1,0:T(8,128)(2,1)}, u32[]{:S(2)}, u32[]{:S(2)}) %collective-permute-start.3) | collective-permute-done | bytes 1605664 | tf_op jit(solution)/shard_map/ppermute | solution.py:247
  343.5 13.7 %products.7 = bf16[8,4,2,32,512]{4,3,2,1,0:T(8,128)(2,1)} custom-call(s32[1]{0:T(128)} %bitcast.half_ref, bf16[4,2,256,256]{3,2,1,0:T(8,128)(2,1)} %get-tuple-element.25.own_ref, bf16[4,784,256]{2,1,0:T(8,128)(2,1)} %get-tuple-element.26.sent_ref, bf16[4,784,256]{2,1,0:T(8,128)(2,1)} %collective-permute-done.3.got_ref), custom_call_target="tpu_custom_call" | custom-call | flops 6442450944 | bytes 5242880 | tf_op jit(solution)/shard_map/products/pallas_call | solution.py:213
  358.6 6.3 %all-to-all-start.7 = ((bf16[8,4,2,32,512]{4,3,2,1,0:T(8,128)(2,1)}), bf16[8,4,2,32,512]{4,3,2,1,0:T(8,128)(2,1)}, u32[]{:S(2)}, u32[]{:S(2)}) async-start(bf16[8,4,2,32,512]{4,3,2,1,0:T(8,128)(2,1)} %products.7), calls=%async_computation.7 | async-start | bytes 4194304 | tf_op jit(solution)/shard_map/all_to_all | solution.py:249
  364.9 5.3 pack.6
  372.0 85.9 %collective-permute-done.2.got_ref = bf16[5,784,256]{2,1,0:T(8,128)(2,1)S(1)} collective-permute-done((bf16[5,784,256]{2,1,0:T(8,128)(2,1)}, bf16[5,784,256]{2,1,0:T(8,128)(2,1)S(1)}, u32[]{:S(2)}, u32[]{:S(2)}) %collective-permute-start.2) | collective-permute-done | bytes 2007072 | tf_op jit(solution)/shard_map/ppermute | solution.py:247
  459.2 16.6 %products.6 = bf16[8,5,2,32,512]{4,3,2,1,0:T(8,128)(2,1)} custom-call(s32[1]{0:T(128)} %bitcast.half_ref, bf16[5,2,256,256]{3,2,1,0:T(8,128)(2,1)} %get-tuple-element.22.own_ref, bf16[5,784,256]{2,1,0:T(8,128)(2,1)} %get-tuple-element.23.sent_ref, bf16[5,784,256]{2,1,0:T(8,128)(2,1)} %copy-done.4), custom_call_target="tpu_custom_call" | custom-call | flops 8053063680 | bytes 6553600 | tf_op jit(solution)/shard_map/products/pallas_call | solution.py:213
  475.8 36.7 %all_to_all.42 = bf16[8,5,2,32,512]{4,3,2,1,0:T(8,128)(2,1)} all-to-all(bf16[8,5,2,32,512]{4,3,2,1,0:T(8,128)(2,1)} %products.6), channel_id=1, replica_groups=mesh['lines'=2,'half'=2,'member'=8] {'member'}, dimensions={0} | all-to-all | bytes 5242880 | tf_op jit(solution)/shard_map/all_to_all | solution.py:249
  512.5 15.1 %restore.1 = bf16[32,512,512]{2,1,0:T(8,128)(2,1)} custom-call(bf16[48,32,512]{2,1,0:T(8,128)(2,1)} %bitcast.2.refs_0_, bf16[64,32,512]{2,1,0:T(8,128)(2,1)} %bitcast.10, bf16[80,32,512]{2,1,0:T(8,128)(2,1)} %bitcast.9, bf16[64,32,512]{2,1,0:T(8,128)(2,1)} %bitcast.8.refs_3_, bf16[256,512]{1,0:T(8,128)(2,1)} %constant.14.clone.refs_4_), custom_call_target="tpu_custom_call" | custom-call | flops 4294967296 | bytes 25165824 | tf_op jit(solution)/shard_map/restore/pallas_call | solution.py:104
  (20 shorter events, 12.1 us)
Async XLA Ops:
  10.0 22.5 %all-to-all-start = ((bf16[8,3,2,32,512]{4,3,2,1,0:T(8,128)(2,1)}), bf16[8,3,2,32,512]{4,3,2,1,0:T(8,128)(2,1)S(1)}, u32[]{:S(2)}, u32[]{:S(2)}) async-start(bf16[8,3,2,32,512]{4,3,2,1,0:T(8,128)(2,1)} %bitcast.11), calls=%async_computation | async-start | bytes 3145728 | tf_op jit(solution)/shard_map/all_to_all | solution.py:245
  32.5 30.8 %copy-start.2 = (bf16[8,3,2,32,512]{4,3,2,1,0:T(8,128)(2,1)}, bf16[8,3,2,32,512]{4,3,2,1,0:T(8,128)(2,1)S(1)}, u32[]{:S(2)}) copy-start(bf16[8,3,2,32,512]{4,3,2,1,0:T(8,128)(2,1)S(1)} %all-to-all-done.mine_ref) | copy-start | bytes 4718596
  32.5 30.8 %copy-start.3 = (bf16[64,32,512]{2,1,0:T(8,128)(2,1)S(1)}, bf16[64,32,512]{2,1,0:T(8,128)(2,1)}, u32[]{:S(2)}) copy-start(bf16[64,32,512]{2,1,0:T(8,128)(2,1)} %get-tuple-element.24) | copy-start | bytes 6291460
  92.4 73.9 %all-to-all-start.4 = ((bf16[8,5,2,32,512]{4,3,2,1,0:T(8,128)(2,1)}), bf16[8,5,2,32,512]{4,3,2,1,0:T(8,128)(2,1)S(1)}, u32[]{:S(2)}, u32[]{:S(2)}) async-start(bf16[8,5,2,32,512]{4,3,2,1,0:T(8,128)(2,1)} %bitcast.12), calls=%async_computation.4 | async-start | bytes 5242880 | tf_op jit(solution)/shard_map/all_to_all | solution.py:245
  101.6 53.9 %collective-permute-start = (bf16[3,784,256]{2,1,0:T(8,128)(2,1)}, bf16[3,784,256]{2,1,0:T(8,128)(2,1)}, u32[]{:S(2)}, u32[]{:S(2)}) collective-permute-start(bf16[3,784,256]{2,1,0:T(8,128)(2,1)} %get-tuple-element.17.sent_ref), channel_id=1, source_target_pairs={{0,8},{8,0},{1,9},{9,1},{2,10},{10,2},{3,11},{11,3},{4,12},{12,4},... | collective-permute-start | bytes 3612680 | tf_op jit(solution)/shard_map/ppermute | solution.py:247
  166.4 10.4 %copy-start = (bf16[8,5,2,32,512]{4,3,2,1,0:T(8,128)(2,1)}, bf16[8,5,2,32,512]{4,3,2,1,0:T(8,128)(2,1)S(1)}, u32[]{:S(2)}) copy-start(bf16[8,5,2,32,512]{4,3,2,1,0:T(8,128)(2,1)S(1)} %all-to-all-done.4.mine_ref) | copy-start | bytes 7864324
  166.4 96.0 %all-to-all-start.1 = ((bf16[8,3,2,32,512]{4,3,2,1,0:T(8,128)(2,1)}), bf16[8,3,2,32,512]{4,3,2,1,0:T(8,128)(2,1)}, u32[]{:S(2)}, u32[]{:S(2)}) async-start(bf16[8,3,2,32,512]{4,3,2,1,0:T(8,128)(2,1)} %products.4), calls=%async_computation.1 | async-start | bytes 3145728 | tf_op jit(solution)/shard_map/all_to_all | solution.py:249
  176.8 70.7 %collective-permute-start.1 = (bf16[4,784,256]{2,1,0:T(8,128)(2,1)}, bf16[4,784,256]{2,1,0:T(8,128)(2,1)S(1)}, u32[]{:S(2)}, u32[]{:S(2)}) collective-permute-start(bf16[4,784,256]{2,1,0:T(8,128)(2,1)} %get-tuple-element.20.sent_ref), channel_id=1, source_target_pairs={{0,8},{8,0},{1,9},{9,1},{2,10},{10,2},{3,11},{11,3},{4,12},{12,4},... | collective-permute-start | bytes 4816904 | tf_op jit(solution)/shard_map/ppermute | solution.py:247
  247.5 1.2 copy-start.5
  262.4 94.8 %all-to-all-start.3 = ((bf16[8,4,2,32,512]{4,3,2,1,0:T(8,128)(2,1)}), bf16[8,4,2,32,512]{4,3,2,1,0:T(8,128)(2,1)S(1)}, u32[]{:S(2)}, u32[]{:S(2)}) async-start(bf16[8,4,2,32,512]{4,3,2,1,0:T(8,128)(2,1)} %products.5), calls=%async_computation.3 | async-start | bytes 4194304 | tf_op jit(solution)/shard_map/all_to_all | solution.py:249
  272.4 71.1 %collective-permute-start.3 = (bf16[4,784,256]{2,1,0:T(8,128)(2,1)}, bf16[4,784,256]{2,1,0:T(8,128)(2,1)}, u32[]{:S(2)}, u32[]{:S(2)}) collective-permute-start(bf16[4,784,256]{2,1,0:T(8,128)(2,1)} %get-tuple-element.26.sent_ref), channel_id=1, source_target_pairs={{0,8},{8,0},{1,9},{9,1},{2,10},{10,2},{3,11},{11,3},{4,12},{12,4},... | collective-permute-start | bytes 4816904 | tf_op jit(solution)/shard_map/ppermute | solution.py:247
  357.2 1.3 copy-start.1
  358.6 117.3 %all-to-all-start.7 = ((bf16[8,4,2,32,512]{4,3,2,1,0:T(8,128)(2,1)}), bf16[8,4,2,32,512]{4,3,2,1,0:T(8,128)(2,1)}, u32[]{:S(2)}, u32[]{:S(2)}) async-start(bf16[8,4,2,32,512]{4,3,2,1,0:T(8,128)(2,1)} %products.7), calls=%async_computation.7 | async-start | bytes 4194304 | tf_op jit(solution)/shard_map/all_to_all | solution.py:249
  370.1 87.8 %collective-permute-start.2 = (bf16[5,784,256]{2,1,0:T(8,128)(2,1)}, bf16[5,784,256]{2,1,0:T(8,128)(2,1)S(1)}, u32[]{:S(2)}, u32[]{:S(2)}) collective-permute-start(bf16[5,784,256]{2,1,0:T(8,128)(2,1)} %get-tuple-element.23.sent_ref), channel_id=1, source_target_pairs={{0,8},{8,0},{1,9},{9,1},{2,10},{10,2},{3,11},{11,3},{4,12},{12,4},... | collective-permute-start | bytes 6021128 | tf_op jit(solution)/shard_map/ppermute | solution.py:247
  457.9 1.3 copy-start.4
